TPU v7x, 1024 devices: a whole 4x8x16 slice. The times are simulated.
1024 devices in a mesh: dp: 32 (over z, core), space: 32 (over x, y).
Axes of the slice: x: 4, y: 8, z: 16, core: 2. Of those that a mesh axis runs over, the one named last changes fastest.
Arguments:
- cotangent: bfloat16 [32, 24, 1024, 1024], P('dp', None, 'space'), may hold values from -6 to 6
- spectrum: float32 [64, 32, 24, 128], P('space', 'dp'), may hold values from -6 to 6
- weights: float32 [64, 24, 24, 128], P('space'), may hold values from -0.875 to 0.875
Outputs:
- grad_input: bfloat16 [32, 24, 1024, 1024], P('dp', None, 'space')
- grad_weights: float32 [64, 576, 128], P('space', 'dp')
All inputs are finite; a program needn't handle non-finite values.
Results may differ from a plain program's by a relative error of at most 0.001.
Values sent between devices are 32-bit elements; how exact they have to be, the bound alone decides.
No kernel may reach another device: no remote copies, remote signals or barrier semaphores. Data moves between devices by JAX's collectives and lax.ppermute only.
A program may use at most 32 MiB of HBM per device.

v0:
```python
import math

import jax
import jax.numpy as jnp
from jax import lax
from jax.sharding import PartitionSpec as P


def column_basis(col_count, modes_y):
    position = jnp.arange(col_count, dtype=jnp.int32)
    frequency = jnp.arange(modes_y, dtype=jnp.int32)
    phase = position[:, None] * frequency[None, :] % col_count
    angles = phase.astype(jnp.float32) * (2.0 * math.pi / col_count)
    return jnp.concatenate([jnp.cos(angles), -jnp.sin(angles)], axis=1)


def row_basis(mode_count, first_row, row_count, height):
    frequency = jnp.arange(mode_count, dtype=jnp.int32)
    position = first_row + jnp.arange(row_count, dtype=jnp.int32)
    phase = frequency[:, None] * position[None, :] % height
    angles = phase.astype(jnp.float32) * (2.0 * math.pi / height)
    return (jnp.cos(angles), jnp.sin(angles))


def spectral_backward(spec_grad, weights, modes_y):
    hp = lax.Precision.HIGHEST
    grad_re, grad_im = (spec_grad[..., :modes_y], spec_grad[..., modes_y:])
    weight_re, weight_im = (weights[..., :modes_y], weights[..., modes_y:])
    real_part = jnp.einsum("kbox,kcox->kbcx", grad_re, weight_re, precision=hp) + jnp.einsum(
        "kbox,kcox->kbcx", grad_im, weight_im, precision=hp
    )
    imag_part = jnp.einsum("kbox,kcox->kbcx", grad_im, weight_re, precision=hp) - jnp.einsum(
        "kbox,kcox->kbcx", grad_re, weight_im, precision=hp
    )
    return jnp.concatenate([real_part, imag_part], axis=-1)


def weight_terms(spectrum, spec_grad, modes_y):
    hp = lax.Precision.HIGHEST
    spec_re, spec_im = (spectrum[..., :modes_y], spectrum[..., modes_y:])
    grad_re, grad_im = (spec_grad[..., :modes_y], spec_grad[..., modes_y:])
    real_part = jnp.einsum("kbcx,kbox->kcox", spec_re, grad_re, precision=hp) + jnp.einsum(
        "kbcx,kbox->kcox", spec_im, grad_im, precision=hp
    )
    imag_part = jnp.einsum("kbcx,kbox->kcox", spec_re, grad_im, precision=hp) - jnp.einsum(
        "kbcx,kbox->kcox", spec_im, grad_re, precision=hp
    )
    joined = jnp.concatenate([real_part, imag_part], axis=-1)
    return joined.reshape(joined.shape[0], joined.shape[1] * joined.shape[2], joined.shape[3])


def body(cotangent, spectrum, weights):
    hp = lax.Precision.HIGHEST
    space_count = lax.axis_size("space")
    raster_count, channels, row_count, col_count = cotangent.shape
    local_modes = spectrum.shape[0]
    modes_y = spectrum.shape[3] // 2
    height = row_count * space_count
    basis = column_basis(col_count, modes_y)
    first_row = lax.axis_index("space") * row_count
    col_spec = jnp.einsum(
        "rcxw,wj->rcxj", cotangent, basis, precision=hp, preferred_element_type=jnp.float32
    )
    forward_scale = 1.0 / math.sqrt(height * col_count)
    cosines, sines = row_basis(local_modes * lax.axis_size("space"), first_row, row_count, height)
    with_cos = jnp.einsum("kx,rcxj->krcj", cosines, col_spec, precision=hp)
    with_sin = jnp.einsum("kx,rcxj->krcj", sines, col_spec, precision=hp)
    joined = jnp.concatenate(
        [
            with_cos[..., :modes_y] + with_sin[..., modes_y:],
            with_cos[..., modes_y:] - with_sin[..., :modes_y],
        ],
        axis=-1,
    )
    spec_grad = lax.psum_scatter(joined * forward_scale, "space", scatter_dimension=0, tiled=True)
    input_spec = spectral_backward(spec_grad, weights, modes_y)
    local_terms = weight_terms(spectrum, spec_grad, modes_y)
    grad_weights = lax.psum_scatter(local_terms, "dp", scatter_dimension=1, tiled=True)
    shard_piece = lax.all_gather(input_spec, "space", axis=0, tiled=True)
    cosines, sines = row_basis(shard_piece.shape[0], first_row, row_count, height)
    back_cos = jnp.einsum("kx,krcj->rcxj", cosines, shard_piece, precision=hp)
    back_sin = jnp.einsum("kx,krcj->rcxj", sines, shard_piece, precision=hp)
    joined = jnp.concatenate(
        [
            back_cos[..., :modes_y] - back_sin[..., modes_y:],
            back_cos[..., modes_y:] + back_sin[..., :modes_y],
        ],
        axis=-1,
    )
    inverse_scale = 1.0 / math.sqrt(local_modes * space_count * modes_y)
    grad_input = (jnp.einsum("rcxj,wj->rcxw", joined, basis, precision=hp) * inverse_scale).astype(
        jnp.bfloat16
    )
    return (grad_input, grad_weights)


def solution(mesh):
    placed = (
        P("dp", None, "space", None),
        P("space", "dp", None, None),
        P("space", None, None, None),
    )
    return jax.shard_map(
        body,
        mesh=mesh,
        in_specs=placed,
        out_specs=(P("dp", None, "space", None), P("space", "dp", None)),
        check_vma=False,
    )
```

profile of v0, /device:TPU:1, one launch (start us, length us, event | category | flops | bytes accessed | tf_op | source)
XLA Modules:
  0.0 524.3 jit_solution(2765691559746632495)
XLA Ops:
  7.2 0.0 copy-start
  7.2 0.0 reduce-scatter.2.cloned.1.call-start
  7.2 2.1 sine_negate_fusion
  9.3 0.0 copy-done
  9.3 1.5 fusion.3
  10.8 1.0 convolution_bitcast_fusion
  11.8 1.0 convolution_bitcast_fusion.1
  12.8 0.5 slice_add_fusion
  13.2 0.3 maximum_multiply_fusion
  13.5 0.0 copy-start.2
  13.5 0.0 copy-start.1
  13.5 1.3 copy.7
  14.9 0.0 reduce-scatter.2.cloned.1.call-update
  14.9 0.0 all-reduce.3.cloned.1.call-start
  15.0 0.0 copy-done.2
  15.0 0.1 slice_bitcast_fusion.3
  15.1 1.3 dynamic-slice
  17.0 232.5 %reduce-scatter.2.cloned.1.call-done = f32[2,1,24,128]{3,2,1,0:T(8,128)} async-done(((f32[64,1,24,128]{3,2,1,0:T(8,128)}), f32[2,1,24,128]{3,2,1,0:T(8,128)}) %reduce-scatter.2.cloned.1.call-update) | async-done | bytes 24592 | tf_op jit(solution)/shard_map/reduce_scatter | solution.py:75
  249.6 0.9 slice_bitcast_fusion.1
  250.5 0.0 copy-done.1
  250.5 0.5 multiply_reduce_fusion.2
  251.1 0.1 pad_maximum_fusion.1
  251.1 36.0 %all_gather.3 = f32[64,1,24,128]{3,2,1,0:T(8,128)S(1)} all-gather(f32[2,1,24,128]{3,2,1,0:T(8,128)S(1)} %pad_maximum_fusion.1), channel_id=1, replica_groups=mesh['dp'=32,'space'=32] {'space'}, dimensions={0}, use_global_device_ids=true | all-gather | bytes 811008 | tf_op jit(solution)/shard_map/all_gather | solution.py:79
  287.1 0.8 convolution_bitcast_fusion.3
  287.9 0.8 convolution_bitcast_fusion.2
  288.7 0.5 add_bitcast_fusion
  289.2 1.5 pad_maximum_fusion
  290.7 0.0 all-reduce.3.cloned.1.call-update
  290.7 0.3 slice_subtract_fusion.1
  291.0 3.9 fusion.2
  294.9 221.2 %all-reduce.3.cloned.1.call-done = f32[2,576,128]{2,0,1:T(2,128)} async-done(((f32[2,576,128]{2,0,1:T(2,128)}), f32[2,576,128]{2,0,1:T(2,128)}) %all-reduce.3.cloned.1.call-update) | async-done | bytes 589840
  516.1 1.3 constant_dynamic-slice_fusion
  (7 shorter events, 0.1 us)
Async XLA Ops:
  7.2 2.2 copy-start
  7.2 242.4 %reduce-scatter.2.cloned.1.call-start = ((), (), s32[]{:S(2)}) async-start(), calls=%async_computation.1 | async-start | bytes 811008 | tf_op jit(solution)/shard_map/reduce_scatter | solution.py:75
  13.5 1.4 copy-start.2
  13.5 237.0 %copy-start.1 = (f32[2,24,24,128]{3,2,1,0:T(8,128)S(1)}, f32[2,24,24,128]{3,2,1,0:T(8,128)}, u32[]{:S(2)}) copy-start(f32[2,24,24,128]{3,2,1,0:T(8,128)} %param.5) | copy-start | bytes 1769476
  14.9 501.2 %all-reduce.3.cloned.1.call-start = ((), (), s32[]{:S(2)}) async-start(), calls=%async_computation.2 | async-start | bytes 1179648
Sparse Core Ops, SparseCore 0:
  15.0 234.4 reduce-scatter.1
  290.8 225.2 all-reduce.2
where the time goes:
time: 525 us; the launch traced here: 524 us
  waiting for transfers between devices  454 us (86%)
  blocking collectives  36 us (7%)
  between operations  14.9 us (3%)
  matrix products  8.9 us (2%)
  other arithmetic  5.7 us (1%)
    reduce_scatter x1, waiting for transfers between devices, body(): lax.psum_scatter(joined * forward_scale, 'space', scatter_dimension=0, ti...  233 us
    unnamed x3, waiting for transfers between devices  221 us
    all_gather x1, blocking collectives, body(): shard_piece = lax.all_gather(input_spec, 'space', axis=0, tiled=True)  36 us
  transfers between devices with their start and end apart: 2, of which 2 were waited for; matrix products, arithmetic and copies ran while one was open for 1% of the time, Pallas kernels for 0%

commit v1 on v0

v1 whole, which is shorter than its diff:
```python
import math

import jax
import jax.numpy as jnp
import numpy as np
from jax import lax
from jax.sharding import PartitionSpec as P

HP = lax.Precision.HIGHEST


def column_basis(col_count, modes_y):
    phase = np.arange(col_count)[:, None] * np.arange(modes_y)[None, :] % col_count
    angles = phase * (2.0 * math.pi / col_count)
    return np.concatenate([np.cos(angles), -np.sin(angles)], axis=1).astype(np.float32)


def row_basis(mode_count, first_row, row_count, height):
    frequency = jnp.arange(mode_count, dtype=jnp.int32)
    position = first_row + jnp.arange(row_count, dtype=jnp.int32)
    phase = frequency[:, None] * position[None, :] % height
    angles = phase.astype(jnp.float32) * (2.0 * math.pi / height)
    return (jnp.cos(angles), jnp.sin(angles))


def input_spectrum(spec_grad, weights, modes_y):
    grad_re, grad_im = spec_grad[..., :modes_y], spec_grad[..., modes_y:]
    weight_re, weight_im = weights[..., :modes_y], weights[..., modes_y:]
    re, im = grad_re[:, None], grad_im[:, None]
    real_part = jnp.sum(re * weight_re + im * weight_im, axis=2)
    imag_part = jnp.sum(im * weight_re - re * weight_im, axis=2)
    return jnp.concatenate([real_part, imag_part], axis=-1)


def to_points(spectrum, owners, modes_y):
    modes, channels, _ = spectrum.shape
    split = spectrum.reshape(modes, channels, 2, owners, modes_y // owners)
    return split.transpose(3, 0, 4, 2, 1).reshape(owners, -1, 2 * channels)


def weight_gradient(spectrum_points, grad_points, channels):
    spec_re, spec_im = spectrum_points[..., :channels], spectrum_points[..., channels:]
    grad_re, grad_im = grad_points[..., :channels], grad_points[..., channels:]

    def product(a, b):
        return jnp.einsum("bpc,bpo->pco", a, b, precision=HP)

    real_part = product(spec_re, grad_re) + product(spec_im, grad_im)
    imag_part = product(spec_re, grad_im) - product(spec_im, grad_re)
    return jnp.stack([real_part, imag_part], axis=1)


def body(cotangent, spectrum, weights):
    space_count, dp_count = lax.axis_size("space"), lax.axis_size("dp")
    _, channels, row_count, col_count = cotangent.shape
    local_modes, modes_y = spectrum.shape[0], spectrum.shape[3] // 2
    height, modes_x = row_count * space_count, local_modes * space_count
    basis = jnp.asarray(column_basis(col_count, modes_y))
    first_row = lax.axis_index("space") * row_count
    cosines, sines = row_basis(modes_x, first_row, row_count, height)

    spectrum_points = lax.all_to_all(
        to_points(spectrum[:, 0], dp_count, modes_y), "dp", 0, 0, tiled=True
    )

    col_spec = jnp.einsum(
        "cxw,wj->cxj", cotangent[0], basis, precision=HP, preferred_element_type=jnp.float32
    )
    with_cos = jnp.einsum("kx,cxj->kcj", cosines, col_spec, precision=HP)
    with_sin = jnp.einsum("kx,cxj->kcj", sines, col_spec, precision=HP)
    partial = jnp.concatenate(
        [
            with_cos[..., :modes_y] + with_sin[..., modes_y:],
            with_cos[..., modes_y:] - with_sin[..., :modes_y],
        ],
        axis=-1,
    ) * (1.0 / math.sqrt(height * col_count))
    partial = lax.all_to_all(partial, "space", 0, 0, tiled=True)
    spec_grad = jnp.sum(partial.reshape(space_count, local_modes, channels, 2 * modes_y), axis=0)

    input_spec = input_spectrum(spec_grad, weights, modes_y)
    everyone = jnp.broadcast_to(input_spec[None], (space_count,) + input_spec.shape)
    all_spec = lax.all_to_all(everyone, "space", 0, 0, tiled=True)
    all_spec = all_spec.reshape(modes_x, channels, 2 * modes_y)

    grad_points = lax.all_to_all(to_points(spec_grad, dp_count, modes_y), "dp", 0, 0, tiled=True)
    terms = weight_gradient(spectrum_points, grad_points, channels)
    pairs = channels * channels // dp_count
    terms = terms.reshape(-1, dp_count, pairs).transpose(1, 0, 2)
    terms = lax.all_to_all(terms, "dp", 0, 0, tiled=True)
    terms = terms.reshape(dp_count, local_modes, modes_y // dp_count, 2, pairs)
    grad_weights = terms.transpose(1, 4, 3, 0, 2).reshape(local_modes, pairs, 2 * modes_y)

    back_cos = jnp.einsum("kx,kcj->cxj", cosines, all_spec, precision=HP)
    back_sin = jnp.einsum("kx,kcj->cxj", sines, all_spec, precision=HP)
    back = jnp.concatenate(
        [
            back_cos[..., :modes_y] - back_sin[..., modes_y:],
            back_cos[..., modes_y:] + back_sin[..., :modes_y],
        ],
        axis=-1,
    )
    inverse_scale = 1.0 / math.sqrt(modes_x * modes_y)
    grad_input = jnp.einsum("cxj,wj->cxw", back, basis, precision=HP) * inverse_scale
    return (grad_input.astype(jnp.bfloat16)[None], grad_weights)


def solution(mesh):
    return jax.shard_map(
        body,
        mesh=mesh,
        in_specs=(
            P("dp", None, "space", None),
            P("space", "dp", None, None),
            P("space", None, None, None),
        ),
        out_specs=(P("dp", None, "space", None), P("space", "dp", None)),
        check_vma=False,
    )
```

time: 525 us -> 144 us (0.27)
  the two profiles are of different devices: /device:TPU:1 before, /device:TPU:8 now
where the time goes in v1:
time: 144 us; the launch traced here: 143 us
  waiting for transfers between devices  74 us (51%)
  starting transfers between devices  44.7 us (31%)
  matrix products  10.5 us (7%)
  local copies, waits for them, and re-layouts  9.2 us (6%)
  other arithmetic  3.74 us (3%)
    all_to_all x1, waiting for transfers between devices, body(): partial = lax.all_to_all(partial, 'space', 0, 0, tiled=True)  21.1 us
    all_to_all x1, waiting for transfers between devices, body(): all_spec = lax.all_to_all(everyone, 'space', 0, 0, tiled=True)  21 us
    all_to_all x1, starting transfers between devices, body(): lax.all_to_all(to_points(spectrum[:, 0], dp_count, modes_y), 'dp', 0, 0,...  19.1 us
    all_to_all x1, waiting for transfers between devices, body(): terms = lax.all_to_all(terms, 'dp', 0, 0, tiled=True)  12.9 us
    all_to_all x1, waiting for transfers between devices, body(): lax.all_to_all(to_points(spec_grad, dp_count, modes_y), 'dp', 0, 0, tiled...  12.6 us
    all_to_all x1, starting transfers between devices, body(): partial = lax.all_to_all(partial, 'space', 0, 0, tiled=True)  10.2 us
    all_to_all x1, waiting for transfers between devices, body(): lax.all_to_all(to_points(spectrum[:, 0], dp_count, modes_y), 'dp', 0, 0,...  6.48 us
    all_to_all x1, starting transfers between devices, body(): lax.all_to_all(to_points(spec_grad, dp_count, modes_y), 'dp', 0, 0, tiled...  6.4 us
  transfers between devices with their start and end apart: 5, of which 5 were waited for; matrix products, arithmetic and copies ran while one was open for 7% of the time, Pallas kernels for 0%

profile of v1, /device:TPU:8, one launch (start us, length us, event | category | flops | bytes accessed | tf_op | source)
XLA Modules:
  0.0 143.1 jit_solution(2084076370324358747)
XLA Ops:
  0.6 1.0 copy.43
  1.8 0.7 reshape.48
  2.5 19.1 %all-to-all-start.3 = ((f32[32,1,192]{2,1,0:T(1,128)}), f32[32,1,192]{2,1,0:T(1,128)S(1)}, u32[]{:S(2)}, u32[]{:S(2)}) async-start(f32[32,1,192]{2,1,0:T(1,128)} %reshape.48), calls=%async_computation.3 | async-start | bytes 65536 | tf_op jit(solution)/shard_map/all_to_all | solution.py:62
  21.7 2.5 %fusion.3 = f32[24,32,128]{2,1,0:T(8,128)S(1)} fusion(f32[1024,128,1]{1,0,2:T(8,128)} %constant.35, bf16[1,24,32,1024]{3,2,1,0:T(8,128)(2,1)S(1)} %copy-done), kind=kOutput, calls=%fused_computation.4 | convolution fusion | flops 1207959552 | bytes 2490368 | tf_op jit(solution)/shard_map/cxw,wj->cxj/dot_general | solution.py:66
  24.2 1.0 fusion.15
  25.2 1.0 fusion.18
  26.1 0.5 slice_add_fusion
  26.6 0.3 maximum_multiply_fusion
  26.9 1.3 copy.33
  28.2 6.5 %all-to-all-done.3 = f32[32,1,192]{2,1,0:T(1,128)S(1)} async-done(((f32[32,1,192]{2,1,0:T(1,128)}), f32[32,1,192]{2,1,0:T(1,128)S(1)}, u32[]{:S(2)}, u32[]{:S(2)}) %all-to-all-start.3) | async-done | bytes 24608 | tf_op jit(solution)/shard_map/all_to_all | solution.py:62
  34.7 10.2 %all-to-all-start = ((f32[64,24,128]{2,1,0:T(8,128)}), f32[64,24,128]{2,1,0:T(8,128)S(1)}, u32[]{:S(2)}, u32[]{:S(2)}) async-start(f32[64,24,128]{2,1,0:T(8,128)} %copy.33), calls=%async_computation | async-start | bytes 1572864 | tf_op jit(solution)/shard_map/all_to_all | solution.py:78
  44.9 0.5 broadcast.31
  45.4 0.7 reduce.1
  46.5 21.1 %all-to-all-done = f32[64,24,128]{2,1,0:T(8,128)S(1)} async-done(((f32[64,24,128]{2,1,0:T(8,128)}), f32[64,24,128]{2,1,0:T(8,128)S(1)}, u32[]{:S(2)}, u32[]{:S(2)}) %all-to-all-start) | async-done | bytes 786464 | tf_op jit(solution)/shard_map/all_to_all | solution.py:78
  68.0 0.8 reshape.46
  68.8 6.4 %all-to-all-start.2 = ((f32[32,1,192]{2,1,0:T(1,128)}), f32[32,1,192]{2,1,0:T(1,128)S(1)}, u32[]{:S(2)}, u32[]{:S(2)}) async-start(f32[32,1,192]{2,1,0:T(1,128)} %reshape.46), calls=%async_computation.2 | async-start | bytes 65536 | tf_op jit(solution)/shard_map/all_to_all | solution.py:86
  75.2 0.4 add_reduce_fusion
  75.6 12.6 %all-to-all-done.2 = f32[32,1,192]{2,1,0:T(1,128)S(1)} async-done(((f32[32,1,192]{2,1,0:T(1,128)}), f32[32,1,192]{2,1,0:T(1,128)S(1)}, u32[]{:S(2)}, u32[]{:S(2)}) %all-to-all-start.2) | async-done | bytes 24608 | tf_op jit(solution)/shard_map/all_to_all | solution.py:86
  88.2 0.7 reduce
  90.5 0.8 reshape.50
  91.3 3.9 %all-to-all-start.4 = ((f32[32,1,144]{2,1,0:T(1,128)}), f32[32,1,144]{2,1,0:T(1,128)S(1)}, u32[]{:S(2)}, u32[]{:S(2)}) async-start(f32[32,1,144]{2,1,0:T(1,128)} %reshape.50), calls=%async_computation.4 | async-start | bytes 65536 | tf_op jit(solution)/shard_map/all_to_all | solution.py:90
  95.3 12.9 %all-to-all-done.4 = f32[32,1,144]{2,1,0:T(1,128)S(1)} async-done(((f32[32,1,144]{2,1,0:T(1,128)}), f32[32,1,144]{2,1,0:T(1,128)S(1)}, u32[]{:S(2)}, u32[]{:S(2)}) %all-to-all-start.4) | async-done | bytes 18464 | tf_op jit(solution)/shard_map/all_to_all | solution.py:90
  108.1 1.1 broadcast_in_dim.4
  109.2 5.1 %all-to-all-start.1 = ((f32[32,2,24,128]{3,1,2,0:T(2,128)}), f32[32,2,24,128]{3,1,2,0:T(2,128)S(1)}, u32[]{:S(2)}, u32[]{:S(2)}) async-start(f32[32,2,24,128]{3,1,2,0:T(2,128)} %broadcast_in_dim.4), calls=%async_computation.1 | async-start | bytes 1572864 | tf_op jit(solution)/shard_map/all_to_all | solution.py:83
  114.3 0.7 reduce.2
  115.4 0.7 copy.53
  116.1 21.0 %all-to-all-done.1 = f32[32,2,24,128]{3,1,2,0:T(2,128)S(1)} async-done(((f32[32,2,24,128]{3,1,2,0:T(2,128)}), f32[32,2,24,128]{3,1,2,0:T(2,128)S(1)}, u32[]{:S(2)}, u32[]{:S(2)}) %all-to-all-start.1) | async-done | bytes 786464 | tf_op jit(solution)/shard_map/all_to_all | solution.py:83
  137.1 0.4 copy.38
  137.6 0.7 convolution_bitcast_fusion.1
  138.3 0.7 convolution_bitcast_fusion
  139.0 0.3 slice_subtract_fusion.1
  139.3 3.8 %fusion.2 = bf16[1,24,32,1024]{3,2,1,0:T(8,128)(2,1)} fusion(f32[1024,128,1]{1,0,2:T(8,128)S(1)} %copy-done.2, f32[24,32,64]{2,1,0:T(8,128)S(1)} %get-tuple-element.13, f32[24,32,64]{2,1,0:T(8,128)S(1)} %get-tuple-element.12), kind=kOutput, calls=%fused_computation.3 | convolution fusion | flops 1209630720 | bytes 2490368 | tf_op jit(solution)/shard_map/cxj,wj->cxw/dot_general | solution.py:104
  (35 shorter events, 3.0 us)
Async XLA Ops:
  0.6 21.1 %copy-start = (bf16[1,24,32,1024]{3,2,1,0:T(8,128)(2,1)S(1)}, bf16[1,24,32,1024]{3,2,1,0:T(8,128)(2,1)}, u32[]{:S(2)}) copy-start(bf16[1,24,32,1024]{3,2,1,0:T(8,128)(2,1)} %param.4) | copy-start | bytes 4718596
  2.5 32.2 %all-to-all-start.3 = ((f32[32,1,192]{2,1,0:T(1,128)}), f32[32,1,192]{2,1,0:T(1,128)S(1)}, u32[]{:S(2)}, u32[]{:S(2)}) async-start(f32[32,1,192]{2,1,0:T(1,128)} %reshape.48), calls=%async_computation.3 | async-start | bytes 65536 | tf_op jit(solution)/shard_map/all_to_all | solution.py:62
  28.2 47.0 %copy-start.1 = (f32[2,24,24,128]{3,2,1,0:T(8,128)S(1)}, f32[2,24,24,128]{3,2,1,0:T(8,128)}, u32[]{:S(2)}) copy-start(f32[2,24,24,128]{3,2,1,0:T(8,128)} %param.6) | copy-start | bytes 1769476
  34.7 32.9 %all-to-all-start = ((f32[64,24,128]{2,1,0:T(8,128)}), f32[64,24,128]{2,1,0:T(8,128)S(1)}, u32[]{:S(2)}, u32[]{:S(2)}) async-start(f32[64,24,128]{2,1,0:T(8,128)} %copy.33), calls=%async_computation | async-start | bytes 1572864 | tf_op jit(solution)/shard_map/all_to_all | solution.py:78
  68.8 19.4 %all-to-all-start.2 = ((f32[32,1,192]{2,1,0:T(1,128)}), f32[32,1,192]{2,1,0:T(1,128)S(1)}, u32[]{:S(2)}, u32[]{:S(2)}) async-start(f32[32,1,192]{2,1,0:T(1,128)} %reshape.46), calls=%async_computation.2 | async-start | bytes 65536 | tf_op jit(solution)/shard_map/all_to_all | solution.py:86
  91.3 16.8 %all-to-all-start.4 = ((f32[32,1,144]{2,1,0:T(1,128)}), f32[32,1,144]{2,1,0:T(1,128)S(1)}, u32[]{:S(2)}, u32[]{:S(2)}) async-start(f32[32,1,144]{2,1,0:T(1,128)} %reshape.50), calls=%async_computation.4 | async-start | bytes 65536 | tf_op jit(solution)/shard_map/all_to_all | solution.py:90
  109.2 27.9 %all-to-all-start.1 = ((f32[32,2,24,128]{3,1,2,0:T(2,128)}), f32[32,2,24,128]{3,1,2,0:T(2,128)S(1)}, u32[]{:S(2)}, u32[]{:S(2)}) async-start(f32[32,2,24,128]{3,1,2,0:T(2,128)} %broadcast_in_dim.4), calls=%async_computation.1 | async-start | bytes 1572864 | tf_op jit(solution)/shard_map/all_to_all | solution.py:83
  138.3 1.0 copy-start.2

commit v2 on v1

--- a/solution.py
+++ b/solution.py
@@ -32,22 +32,40 @@
     return jnp.concatenate([real_part, imag_part], axis=-1)
 
 
-def to_points(spectrum, owners, modes_y):
+def weight_terms(spectrum, spec_grad, modes_y, owners):
     modes, channels, _ = spectrum.shape
-    split = spectrum.reshape(modes, channels, 2, owners, modes_y // owners)
-    return split.transpose(3, 0, 4, 2, 1).reshape(owners, -1, 2 * channels)
+    spec_re, spec_im = spectrum[:, :, None, :modes_y], spectrum[:, :, None, modes_y:]
+    grad_re, grad_im = spec_grad[:, None, :, :modes_y], spec_grad[:, None, :, modes_y:]
+    real_part = spec_re * grad_re + spec_im * grad_im
+    imag_part = spec_re * grad_im - spec_im * grad_re
+    terms = jnp.concatenate([real_part, imag_part], axis=-1)
+    pairs = channels * channels // owners
+    terms = terms.reshape(modes, owners, pairs, 2 * modes_y).transpose(1, 0, 2, 3)
+    return terms.reshape(owners, modes * pairs, 2 * modes_y)
 
 
-def weight_gradient(spectrum_points, grad_points, channels):
-    spec_re, spec_im = spectrum_points[..., :channels], spectrum_points[..., channels:]
-    grad_re, grad_im = grad_points[..., :channels], grad_points[..., channels:]
+def shift_dp(x, hop, chips):
+    pairs = [(2 * z + c, 2 * ((z + hop) % chips) + c) for z in range(chips) for c in range(2)]
+    return lax.ppermute(x, "dp", pairs)
 
-    def product(a, b):
-        return jnp.einsum("bpc,bpo->pco", a, b, precision=HP)
 
-    real_part = product(spec_re, grad_re) + product(spec_im, grad_im)
-    imag_part = product(spec_re, grad_im) - product(spec_im, grad_re)
-    return jnp.stack([real_part, imag_part], axis=1)
+def sum_to_owners(terms, chips):
+    index = lax.axis_index("dp")
+    core, z = index % 2, index // 2
+    by_core = terms.reshape((chips, 2) + terms.shape[1:])
+    mine = lax.dynamic_index_in_dim(by_core, core, 1, keepdims=False)
+    other = lax.dynamic_index_in_dim(by_core, 1 - core, 1, keepdims=False)
+    mine = mine + lax.ppermute(other, "dp", [(i, i ^ 1) for i in range(2 * chips)])
+    ahead = lax.dynamic_slice_in_dim(jnp.concatenate([mine, mine]), z, chips)
+    groups = ahead.reshape((chips // 4, 4) + ahead.shape[1:])
+    near = groups[:, 0]
+    behind = jnp.concatenate([groups[-1:, 3], groups[:-1, 3]])
+    for part, hop in ((groups[:, 1], 1), (behind, -1), (groups[:, 2], 2)):
+        near = near + shift_dp(part, hop, chips)
+    total = near[0]
+    for step in range(1, chips // 4):
+        total = total + shift_dp(near[step], 4 * step, chips)
+    return total
 
 
 def body(cotangent, spectrum, weights):
@@ -58,10 +76,6 @@
     basis = jnp.asarray(column_basis(col_count, modes_y))
     first_row = lax.axis_index("space") * row_count
     cosines, sines = row_basis(modes_x, first_row, row_count, height)
-
-    spectrum_points = lax.all_to_all(
-        to_points(spectrum[:, 0], dp_count, modes_y), "dp", 0, 0, tiled=True
-    )
 
     col_spec = jnp.einsum(
         "cxw,wj->cxj", cotangent[0], basis, precision=HP, preferred_element_type=jnp.float32
@@ -83,13 +97,8 @@
     all_spec = lax.all_to_all(everyone, "space", 0, 0, tiled=True)
     all_spec = all_spec.reshape(modes_x, channels, 2 * modes_y)
 
-    grad_points = lax.all_to_all(to_points(spec_grad, dp_count, modes_y), "dp", 0, 0, tiled=True)
-    terms = weight_gradient(spectrum_points, grad_points, channels)
-    pairs = channels * channels // dp_count
-    terms = terms.reshape(-1, dp_count, pairs).transpose(1, 0, 2)
-    terms = lax.all_to_all(terms, "dp", 0, 0, tiled=True)
-    terms = terms.reshape(dp_count, local_modes, modes_y // dp_count, 2, pairs)
-    grad_weights = terms.transpose(1, 4, 3, 0, 2).reshape(local_modes, pairs, 2 * modes_y)
+    terms = weight_terms(spectrum[:, 0], spec_grad, modes_y, dp_count)
+    grad_weights = sum_to_owners(terms, dp_count // 2).reshape(local_modes, -1, 2 * modes_y)
 
     back_cos = jnp.einsum("kx,kcj->cxj", cosines, all_spec, precision=HP)
     back_sin = jnp.einsum("kx,kcj->cxj", sines, all_spec, precision=HP)

time: 144 us -> 111 us (0.77)
  the two profiles are of different devices: /device:TPU:8 before, /device:TPU:2 now
where the time goes in v2:
time: 111 us; the launch traced here: 110 us
  starting transfers between devices  62.8 us (57%)
  waiting for transfers between devices  27.1 us (24%)
  matrix products  9.6 us (9%)
  local copies, waits for them, and re-layouts  6.88 us (6%)
  other arithmetic  2.57 us (2%)
    ppermute x6, starting transfers between devices, shift_dp(): return lax.ppermute(x, 'dp', pairs)  37 us
    all_to_all x1, starting transfers between devices, body(): partial = lax.all_to_all(partial, 'space', 0, 0, tiled=True)  16.9 us
    all_to_all x1, waiting for transfers between devices, body(): partial = lax.all_to_all(partial, 'space', 0, 0, tiled=True)  14.7 us
    ppermute x6, waiting for transfers between devices, shift_dp(): return lax.ppermute(x, 'dp', pairs)  12.4 us
    all_to_all x1, starting transfers between devices, body(): all_spec = lax.all_to_all(everyone, 'space', 0, 0, tiled=True)  6.9 us
    dot_general x1, matrix products, body(): jnp.einsum('cxj,wj->cxw', back, basis, precision=HP) * inverse_scale  3.78 us
    dot_general x1, matrix products, body(): jnp.einsum('cxw,wj->cxj', cotangent[0], basis, precision=HP, preferred_el...  2.45 us
  transfers between devices with their start and end apart: 9, of which 5 were waited for; matrix products, arithmetic and copies ran while one was open for 2% of the time, Pallas kernels for 0%

profile of v2, /device:TPU:2, one launch (start us, length us, event | category | flops | bytes accessed | tf_op | source)
XLA Modules:
  0.0 109.9 jit_solution(14746573082519454683)
XLA Ops:
  0.7 1.4 %copy-done = bf16[1,24,32,1024]{3,2,1,0:T(8,128)(2,1)S(1)} copy-done((bf16[1,24,32,1024]{3,2,1,0:T(8,128)(2,1)S(1)}, bf16[1,24,32,1024]{3,2,1,0:T(8,128)(2,1)}, u32[]{:S(2)}) %copy-start) | copy-done | bytes 1572888
  2.0 2.4 %fusion.3 = f32[24,32,128]{2,1,0:T(8,128)S(1)} fusion(f32[1024,128,1]{1,0,2:T(8,128)} %constant.71, bf16[1,24,32,1024]{3,2,1,0:T(8,128)(2,1)S(1)} %copy-done), kind=kOutput, calls=%fused_computation.4 | convolution fusion | flops 1207959552 | bytes 2490368 | tf_op jit(solution)/shard_map/cxw,wj->cxj/dot_general | solution.py:80
  4.5 1.0 fusion.17
  5.5 1.0 fusion.20
  6.4 0.5 slice_add_fusion
  6.9 0.3 maximum_multiply_fusion
  7.2 1.3 %copy.19 = f32[64,24,128]{2,1,0:T(8,128)} copy(f32[64,24,128]{2,0,1:T(8,128)S(1)} %maximum_multiply_fusion) | data formatting | bytes 1572864 | tf_op jit(solution)/shard_map/mul | solution.py:85
  8.5 16.9 %all-to-all-start = ((f32[64,24,128]{2,1,0:T(8,128)}), f32[64,24,128]{2,1,0:T(8,128)S(1)}, u32[]{:S(2)}, u32[]{:S(2)}) async-start(f32[64,24,128]{2,1,0:T(8,128)} %copy.19), calls=%async_computation | async-start | bytes 1572864 | tf_op jit(solution)/shard_map/all_to_all | solution.py:92
  25.5 14.7 %all-to-all-done = f32[64,24,128]{2,1,0:T(8,128)S(1)} async-done(((f32[64,24,128]{2,1,0:T(8,128)}), f32[64,24,128]{2,1,0:T(8,128)S(1)}, u32[]{:S(2)}, u32[]{:S(2)}) %all-to-all-start) | async-done | bytes 786464 | tf_op jit(solution)/shard_map/all_to_all | solution.py:92
  40.3 0.5 multiply_add_fusion
  40.9 0.5 copy.25
  41.3 0.5 copy.26
  41.8 0.7 maximum_bitcast_fusion
  42.5 0.6 constant_dynamic-slice_fusion
  43.1 1.9 %collective-permute-start = (f32[16,36,128]{2,0,1:T(8,128)S(1)}, f32[16,36,128]{2,0,1:T(8,128)S(1)}, u32[]{:S(2)}, u32[]{:S(2)}) collective-permute-start(f32[16,36,128]{2,0,1:T(8,128)S(1)} %bitcast.90), channel_id=1, source_target_pairs={{0,32},{32,0},{64,96},{96,64},{128,160},{160,128},{192,224},{224,1... | collective-permute-start | bytes 884744 | tf_op jit(solution)/shard_map/ppermute | solution.py:58
  45.2 1.1 broadcast_in_dim.4
  46.3 6.9 %all-to-all-start.1 = ((f32[32,2,24,128]{3,1,2,0:T(2,128)}), f32[32,2,24,128]{3,1,2,0:T(2,128)S(1)}, u32[]{:S(2)}, u32[]{:S(2)}) async-start(f32[32,2,24,128]{3,1,2,0:T(2,128)} %broadcast_in_dim.4), calls=%async_computation.1 | async-start | bytes 1572864 | tf_op jit(solution)/shard_map/all_to_all | solution.py:97
  53.5 18.2 %collective-permute-start.2 = (f32[4,36,128]{2,0,1:T(4,128)S(1)}, f32[4,36,128]{2,0,1:T(4,128)S(1)}, u32[]{:S(2)}, u32[]{:S(2)}) collective-permute-start(f32[4,36,128]{2,0,1:T(4,128)S(1)} %pad_maximum_fusion), channel_id=1, source_target_pairs={{0,960},{32,992},{64,0},{96,32},{128,64},{160,96},{192,128},{224,1... | collective-permute-start | bytes 221192 | tf_op jit(solution)/shard_map/ppermute | solution.py:49
  71.9 1.9 %collective-permute-start.3 = (f32[4,36,128]{2,0,1:T(4,128)S(1)}, f32[4,36,128]{2,0,1:T(4,128)S(1)}, u32[]{:S(2)}, u32[]{:S(2)}) collective-permute-start(f32[4,36,128]{2,0,1:T(4,128)S(1)} %bitcast.93), channel_id=1, source_target_pairs={{0,128},{32,160},{64,192},{96,224},{128,256},{160,288},{192,320},{... | collective-permute-start | bytes 221192 | tf_op jit(solution)/shard_map/ppermute | solution.py:49
  73.8 1.9 %collective-permute-start.1 = (f32[4,36,128]{2,0,1:T(4,128)S(1)}, f32[4,36,128]{2,0,1:T(4,128)S(1)}, u32[]{:S(2)}, u32[]{:S(2)}) collective-permute-start(f32[4,36,128]{2,0,1:T(4,128)S(1)} %bitcast.92), channel_id=1, source_target_pairs={{0,64},{32,96},{64,128},{96,160},{128,192},{160,224},{192,256},{22... | collective-permute-start | bytes 221192 | tf_op jit(solution)/shard_map/ppermute | solution.py:49
  75.7 5.6 %collective-permute-done.3 = f32[4,36,128]{2,0,1:T(4,128)S(1)} collective-permute-done((f32[4,36,128]{2,0,1:T(4,128)S(1)}, f32[4,36,128]{2,0,1:T(4,128)S(1)}, u32[]{:S(2)}, u32[]{:S(2)}) %collective-permute-start.3) | collective-permute-done | bytes 73760 | tf_op jit(solution)/shard_map/ppermute | solution.py:49
  81.3 0.8 collective-permute-done.1
  82.2 1.9 %collective-permute-start.4 = (f32[36,128]{1,0:T(8,128)S(1)}, f32[36,128]{1,0:T(8,128)S(1)}, u32[]{:S(2)}, u32[]{:S(2)}) collective-permute-start(f32[36,128]{1,0:T(8,128)S(1)} %bitcast.97), channel_id=1, source_target_pairs={{0,256},{32,288},{64,320},{96,352},{128,384},{160,416},{192,448},{... | collective-permute-start | bytes 55304 | tf_op jit(solution)/shard_map/ppermute | solution.py:49
  84.2 9.3 %collective-permute-start.5 = (f32[36,128]{1,0:T(8,128)S(1)}, f32[36,128]{1,0:T(8,128)S(1)}, u32[]{:S(2)}, u32[]{:S(2)}) collective-permute-start(f32[36,128]{1,0:T(8,128)S(1)} %bitcast.98), channel_id=1, source_target_pairs={{0,512},{32,544},{64,576},{96,608},{128,640},{160,672},{192,704},{... | collective-permute-start | bytes 55304 | tf_op jit(solution)/shard_map/ppermute | solution.py:49
  93.5 3.8 %collective-permute-start.6 = (f32[36,128]{1,0:T(8,128)S(1)}, f32[36,128]{1,0:T(8,128)S(1)}, u32[]{:S(2)}, u32[]{:S(2)}) collective-permute-start(f32[36,128]{1,0:T(8,128)S(1)} %bitcast.99), channel_id=1, source_target_pairs={{0,768},{32,800},{64,832},{96,864},{128,896},{160,928},{192,960},{... | collective-permute-start | bytes 55304 | tf_op jit(solution)/shard_map/ppermute | solution.py:49
  97.3 1.3 %collective-permute-done.5 = f32[36,128]{1,0:T(8,128)S(1)} collective-permute-done((f32[36,128]{1,0:T(8,128)S(1)}, f32[36,128]{1,0:T(8,128)S(1)}, u32[]{:S(2)}, u32[]{:S(2)}) %collective-permute-start.5) | collective-permute-done | bytes 18464 | tf_op jit(solution)/shard_map/ppermute | solution.py:49
  98.6 4.7 %collective-permute-done.6 = f32[36,128]{1,0:T(8,128)S(1)} collective-permute-done((f32[36,128]{1,0:T(8,128)S(1)}, f32[36,128]{1,0:T(8,128)S(1)}, u32[]{:S(2)}, u32[]{:S(2)}) %collective-permute-start.6) | collective-permute-done | bytes 18464 | tf_op jit(solution)/shard_map/ppermute | solution.py:49
  103.3 0.6 copy.35
  103.9 0.4 copy.24
  104.3 0.7 convolution_bitcast_fusion.1
  105.1 0.7 convolution_bitcast_fusion
  106.1 3.8 %fusion.2 = bf16[1,24,32,1024]{3,2,1,0:T(8,128)(2,1)} fusion(f32[1024,128,1]{1,0,2:T(8,128)S(1)} %copy-done.2, f32[24,32,64]{2,1,0:T(8,128)S(1)} %get-tuple-element.11, f32[24,32,64]{2,1,0:T(8,128)S(1)} %get-tuple-element.10), kind=kOutput, calls=%fused_computation.3 | convolution fusion | flops 1209630720 | bytes 2490368 | tf_op jit(solution)/shard_map/cxj,wj->cxw/dot_general | solution.py:113
  (32 shorter events, 1.1 us)
Async XLA Ops:
  0.6 1.4 %copy-start = (bf16[1,24,32,1024]{3,2,1,0:T(8,128)(2,1)S(1)}, bf16[1,24,32,1024]{3,2,1,0:T(8,128)(2,1)}, u32[]{:S(2)}) copy-start(bf16[1,24,32,1024]{3,2,1,0:T(8,128)(2,1)} %param.4) | copy-start | bytes 4718596
  8.5 31.7 %copy-start.3 = (f32[2,1,24,128]{3,2,1,0:T(8,128)S(1)}, f32[2,1,24,128]{3,2,1,0:T(8,128)}, u32[]{:S(2)}) copy-start(f32[2,1,24,128]{3,2,1,0:T(8,128)} %param.5) | copy-start | bytes 73732
  8.5 31.8 %copy-start.1 = (f32[2,24,24,128]{3,2,1,0:T(8,128)S(1)}, f32[2,24,24,128]{3,2,1,0:T(8,128)}, u32[]{:S(2)}) copy-start(f32[2,24,24,128]{3,2,1,0:T(8,128)} %param.6) | copy-start | bytes 1769476
  8.5 31.6 %all-to-all-start = ((f32[64,24,128]{2,1,0:T(8,128)}), f32[64,24,128]{2,1,0:T(8,128)S(1)}, u32[]{:S(2)}, u32[]{:S(2)}) async-start(f32[64,24,128]{2,1,0:T(8,128)} %copy.19), calls=%async_computation | async-start | bytes 1572864 | tf_op jit(solution)/shard_map/all_to_all | solution.py:92
  43.1 10.0 %collective-permute-start = (f32[16,36,128]{2,0,1:T(8,128)S(1)}, f32[16,36,128]{2,0,1:T(8,128)S(1)}, u32[]{:S(2)}, u32[]{:S(2)}) collective-permute-start(f32[16,36,128]{2,0,1:T(8,128)S(1)} %bitcast.90), channel_id=1, source_target_pairs={{0,32},{32,0},{64,96},{96,64},{128,160},{160,128},{192,224},{224,1... | collective-permute-start | bytes 884744 | tf_op jit(solution)/shard_map/ppermute | solution.py:58
  46.3 57.7 %all-to-all-start.1 = ((f32[32,2,24,128]{3,1,2,0:T(2,128)}), f32[32,2,24,128]{3,1,2,0:T(2,128)S(1)}, u32[]{:S(2)}, u32[]{:S(2)}) async-start(f32[32,2,24,128]{3,1,2,0:T(2,128)} %broadcast_in_dim.4), calls=%async_computation.1 | async-start | bytes 1572864 | tf_op jit(solution)/shard_map/all_to_all | solution.py:97
  53.5 22.2 %collective-permute-start.2 = (f32[4,36,128]{2,0,1:T(4,128)S(1)}, f32[4,36,128]{2,0,1:T(4,128)S(1)}, u32[]{:S(2)}, u32[]{:S(2)}) collective-permute-start(f32[4,36,128]{2,0,1:T(4,128)S(1)} %pad_maximum_fusion), channel_id=1, source_target_pairs={{0,960},{32,992},{64,0},{96,32},{128,64},{160,96},{192,128},{224,1... | collective-permute-start | bytes 221192 | tf_op jit(solution)/shard_map/ppermute | solution.py:49
  71.9 9.5 %collective-permute-start.3 = (f32[4,36,128]{2,0,1:T(4,128)S(1)}, f32[4,36,128]{2,0,1:T(4,128)S(1)}, u32[]{:S(2)}, u32[]{:S(2)}) collective-permute-start(f32[4,36,128]{2,0,1:T(4,128)S(1)} %bitcast.93), channel_id=1, source_target_pairs={{0,128},{32,160},{64,192},{96,224},{128,256},{160,288},{192,320},{... | collective-permute-start | bytes 221192 | tf_op jit(solution)/shard_map/ppermute | solution.py:49
  73.8 8.3 %collective-permute-start.1 = (f32[4,36,128]{2,0,1:T(4,128)S(1)}, f32[4,36,128]{2,0,1:T(4,128)S(1)}, u32[]{:S(2)}, u32[]{:S(2)}) collective-permute-start(f32[4,36,128]{2,0,1:T(4,128)S(1)} %bitcast.92), channel_id=1, source_target_pairs={{0,64},{32,96},{64,128},{96,160},{128,192},{160,224},{192,256},{22... | collective-permute-start | bytes 221192 | tf_op jit(solution)/shard_map/ppermute | solution.py:49
  82.2 15.1 %collective-permute-start.4 = (f32[36,128]{1,0:T(8,128)S(1)}, f32[36,128]{1,0:T(8,128)S(1)}, u32[]{:S(2)}, u32[]{:S(2)}) collective-permute-start(f32[36,128]{1,0:T(8,128)S(1)} %bitcast.97), channel_id=1, source_target_pairs={{0,256},{32,288},{64,320},{96,352},{128,384},{160,416},{192,448},{... | collective-permute-start | bytes 55304 | tf_op jit(solution)/shard_map/ppermute | solution.py:49
  84.2 14.4 %collective-permute-start.5 = (f32[36,128]{1,0:T(8,128)S(1)}, f32[36,128]{1,0:T(8,128)S(1)}, u32[]{:S(2)}, u32[]{:S(2)}) collective-permute-start(f32[36,128]{1,0:T(8,128)S(1)} %bitcast.98), channel_id=1, source_target_pairs={{0,512},{32,544},{64,576},{96,608},{128,640},{160,672},{192,704},{... | collective-permute-start | bytes 55304 | tf_op jit(solution)/shard_map/ppermute | solution.py:49
  93.5 9.8 %collective-permute-start.6 = (f32[36,128]{1,0:T(8,128)S(1)}, f32[36,128]{1,0:T(8,128)S(1)}, u32[]{:S(2)}, u32[]{:S(2)}) collective-permute-start(f32[36,128]{1,0:T(8,128)S(1)} %bitcast.99), channel_id=1, source_target_pairs={{0,768},{32,800},{64,832},{96,864},{128,896},{160,928},{192,960},{... | collective-permute-start | bytes 55304 | tf_op jit(solution)/shard_map/ppermute | solution.py:49
  105.1 1.0 copy-start.2

commit v3 on v2

--- a/solution.py
+++ b/solution.py
@@ -4,9 +4,11 @@
 import jax.numpy as jnp
 import numpy as np
 from jax import lax
+from jax.sharding import Mesh
 from jax.sharding import PartitionSpec as P
 
 HP = lax.Precision.HIGHEST
+DP = ("far", "near", "core")
 
 
 def column_basis(col_count, modes_y):
@@ -44,32 +46,29 @@
     return terms.reshape(owners, modes * pairs, 2 * modes_y)
 
 
-def shift_dp(x, hop, chips):
-    pairs = [(2 * z + c, 2 * ((z + hop) % chips) + c) for z in range(chips) for c in range(2)]
-    return lax.ppermute(x, "dp", pairs)
+def shift_near(x, hop):
+    near, far = lax.axis_size("near"), lax.axis_size("far")
+    chips = near * far
+    return lax.ppermute(x, ("far", "near"), [(z, (z + hop) % chips) for z in range(chips)])
 
 
-def sum_to_owners(terms, chips):
-    index = lax.axis_index("dp")
-    core, z = index % 2, index // 2
-    by_core = terms.reshape((chips, 2) + terms.shape[1:])
-    mine = lax.dynamic_index_in_dim(by_core, core, 1, keepdims=False)
-    other = lax.dynamic_index_in_dim(by_core, 1 - core, 1, keepdims=False)
-    mine = mine + lax.ppermute(other, "dp", [(i, i ^ 1) for i in range(2 * chips)])
-    ahead = lax.dynamic_slice_in_dim(jnp.concatenate([mine, mine]), z, chips)
-    groups = ahead.reshape((chips // 4, 4) + ahead.shape[1:])
-    near = groups[:, 0]
-    behind = jnp.concatenate([groups[-1:, 3], groups[:-1, 3]])
-    for part, hop in ((groups[:, 1], 1), (behind, -1), (groups[:, 2], 2)):
-        near = near + shift_dp(part, hop, chips)
-    total = near[0]
-    for step in range(1, chips // 4):
-        total = total + shift_dp(near[step], 4 * step, chips)
-    return total
+def sum_to_owners(terms, later):
+    near, far = lax.axis_size("near"), lax.axis_size("far")
+    core, here = lax.axis_index("core"), lax.axis_index("near")
+    by_core = terms.reshape((far, near, 2) + terms.shape[1:])
+    mine = lax.dynamic_index_in_dim(by_core, core, 2, keepdims=False)
+    other = lax.dynamic_index_in_dim(by_core, 1 - core, 2, keepdims=False)
+    mine = mine + lax.ppermute(other, "core", [(0, 1), (1, 0)])
+    ahead = lax.dynamic_slice_in_dim(jnp.concatenate([mine, mine], axis=1), here, near, axis=1)
+    total = ahead[:, 0]
+    for part, hop in ((ahead[:, 1], 1), (ahead[:, near - 1], -1), (ahead[:, 2], 2)):
+        total = total + shift_near(part, hop)
+    total, _ = lax.optimization_barrier((total, later))
+    return jnp.sum(lax.all_to_all(total, "far", 0, 0, tiled=True), axis=0)
 
 
 def body(cotangent, spectrum, weights):
-    space_count, dp_count = lax.axis_size("space"), lax.axis_size("dp")
+    space_count, dp_count = lax.axis_size("space"), lax.axis_size(DP)
     _, channels, row_count, col_count = cotangent.shape
     local_modes, modes_y = spectrum.shape[0], spectrum.shape[3] // 2
     height, modes_x = row_count * space_count, local_modes * space_count
@@ -98,7 +97,7 @@
     all_spec = all_spec.reshape(modes_x, channels, 2 * modes_y)
 
     terms = weight_terms(spectrum[:, 0], spec_grad, modes_y, dp_count)
-    grad_weights = sum_to_owners(terms, dp_count // 2).reshape(local_modes, -1, 2 * modes_y)
+    grad_weights = sum_to_owners(terms, all_spec).reshape(local_modes, -1, 2 * modes_y)
 
     back_cos = jnp.einsum("kx,kcj->cxj", cosines, all_spec, precision=HP)
     back_sin = jnp.einsum("kx,kcj->cxj", sines, all_spec, precision=HP)
@@ -115,14 +114,12 @@
 
 
 def solution(mesh):
+    dp_count, space_count = mesh.devices.shape
+    chips = mesh.devices.reshape(dp_count // 8, 4, 2, space_count)
     return jax.shard_map(
         body,
-        mesh=mesh,
-        in_specs=(
-            P("dp", None, "space", None),
-            P("space", "dp", None, None),
-            P("space", None, None, None),
-        ),
-        out_specs=(P("dp", None, "space", None), P("space", "dp", None)),
+        mesh=Mesh(chips, DP + ("space",)),
+        in_specs=(P(DP, None, "space", None), P("space", DP, None, None), P("space", None, None, None)),
+        out_specs=(P(DP, None, "space", None), P("space", DP, None)),
         check_vma=False,
     )

time: 111 us -> 108 us (0.973)
  the two profiles are of different devices: /device:TPU:2 before, /device:TPU:8 now
where the time goes in v3:
time: 108 us; the launch traced here: 107 us
  starting transfers between devices  34 us (31%)
  blocking collectives  33.3 us (31%)
  waiting for transfers between devices  19.4 us (18%)
  matrix products  9.61 us (9%)
  local copies, waits for them, and re-layouts  6.64 us (6%)
  other arithmetic  3.54 us (3%)
    all_to_all x1, blocking collectives, body(): partial = lax.all_to_all(partial, 'space', 0, 0, tiled=True)  33.3 us
    ppermute x3, starting transfers between devices, shift_near(): lax.ppermute(x, ('far', 'near'), [(z, (z + hop) % chips) for z in range(c...  22.1 us
    all_to_all x1, waiting for transfers between devices, sum_to_owners(): return jnp.sum(lax.all_to_all(total, 'far', 0, 0, tiled=True), axis=0)  10.2 us
    ppermute x3, waiting for transfers between devices, shift_near(): lax.ppermute(x, ('far', 'near'), [(z, (z + hop) % chips) for z in range(c...  7.67 us
    all_to_all x1, starting transfers between devices, sum_to_owners(): return jnp.sum(lax.all_to_all(total, 'far', 0, 0, tiled=True), axis=0)  5.11 us
    all_to_all x1, starting transfers between devices, body(): all_spec = lax.all_to_all(everyone, 'space', 0, 0, tiled=True)  4.92 us
    dot_general x1, matrix products, body(): jnp.einsum('cxj,wj->cxw', back, basis, precision=HP) * inverse_scale  3.79 us
    dot_general x1, matrix products, body(): jnp.einsum('cxw,wj->cxj', cotangent[0], basis, precision=HP, preferred_el...  2.44 us
  transfers between devices with their start and end apart: 6, of which 3 were waited for; matrix products, arithmetic and copies ran while one was open for 7% of the time, Pallas kernels for 0%

profile of v3, /device:TPU:8, one launch (start us, length us, event | category | flops | bytes accessed | tf_op | source)
XLA Modules:
  0.0 107.4 jit_solution(14516291904392655977)
XLA Ops:
  0.7 1.4 %copy-done = bf16[1,24,32,1024]{3,2,1,0:T(8,128)(2,1)S(1)} copy-done((bf16[1,24,32,1024]{3,2,1,0:T(8,128)(2,1)S(1)}, bf16[1,24,32,1024]{3,2,1,0:T(8,128)(2,1)}, u32[]{:S(2)}) %copy-start) | copy-done | bytes 1572888
  2.0 2.4 %fusion.3 = f32[24,32,128]{2,1,0:T(8,128)S(1)} fusion(f32[1024,128,1]{1,0,2:T(8,128)} %constant.60, bf16[1,24,32,1024]{3,2,1,0:T(8,128)(2,1)S(1)} %copy-done), kind=kOutput, calls=%fused_computation.4 | convolution fusion | flops 1207959552 | bytes 2490368 | tf_op jit(solution)/shard_map/cxw,wj->cxj/dot_general | solution.py:79
  4.5 1.0 fusion.16
  5.5 1.0 fusion.19
  6.4 0.5 slice_add_fusion
  6.9 0.3 maximum_multiply_fusion
  7.2 0.5 copy.59
  7.7 33.3 %all_to_all.15 = f32[64,24,128]{2,1,0:T(8,128)S(1)} all-to-all(f32[64,24,128]{2,1,0:T(8,128)S(1)} %copy.59), channel_id=1, replica_groups=mesh['far'=4,'near'=4,'core'=2,'space'=32] {'space'}, dimensions={0} | all-to-all | bytes 1572864 | tf_op jit(solution)/shard_map/all_to_all | solution.py:91
  41.1 1.4 %multiply_add_fusion = (f32[2,24,24,64]{3,2,1,0:T(8,128)}, f32[2,24,24,64]{3,2,1,0:T(8,128)S(1)}, f32[2,24,64]{2,1,0:T(8,128)S(1)}, f32[2,24,64]{2,1,0:T(8,128)S(1)}) fusion(f32[2,24,64]{2,1,0:T(8,128)S(1)} %get-tuple-element.33, f32[2,24,64]{2,1,0:T(8,128)S(1)} %get-tuple-element.32, f32[2,24,64]{2,1,0:T(8,128)S(1)} %get-tuple-element.36, ...), kind=kLoop, calls=%fused_computation.14 | loop fusion | flops 1026048 | bytes 1253376 | tf_op jit(solution)/shard_map/add | solution.py:41
  42.6 1.1 %broadcast_in_dim.4 = f32[32,2,24,128]{3,1,2,0:T(2,128)} broadcast(f32[2,24,128]{2,0,1:T(2,128)S(1)} %copy.63), dimensions={1,2,3} | broadcast | bytes 811008 | tf_op jit(solution)/shard_map/broadcast_in_dim | solution.py:95
  43.6 4.9 %all-to-all-start.1 = ((f32[32,2,24,128]{3,1,2,0:T(2,128)}), f32[32,2,24,128]{3,1,2,0:T(2,128)S(1)}, u32[]{:S(2)}, u32[]{:S(2)}) async-start(f32[32,2,24,128]{3,1,2,0:T(2,128)} %broadcast_in_dim.4), calls=%async_computation.1 | async-start | bytes 1572864 | tf_op jit(solution)/shard_map/all_to_all | solution.py:96
  48.6 0.5 copy.65
  49.0 0.5 copy.66
  49.5 0.7 maximum_bitcast_fusion
  50.3 0.6 constant_dynamic-slice_fusion.1
  50.9 1.9 %collective-permute-start = (f32[4,4,36,128]{3,1,2,0:T(4,128)S(1)}, f32[4,4,36,128]{3,1,2,0:T(4,128)S(1)}, u32[]{:S(2)}, u32[]{:S(2)}) collective-permute-start(f32[4,4,36,128]{3,1,2,0:T(4,128)S(1)} %bitcast.64), channel_id=1, source_target_pairs={{0,32},{32,0},{1,33},{33,1},{2,34},{34,2},{3,35},{35,3},{4,36},{36... | collective-permute-start | bytes 884744 | tf_op jit(solution)/shard_map/ppermute | solution.py:61
  52.9 1.5 %collective-permute-done = f32[4,4,36,128]{3,1,2,0:T(4,128)S(1)} collective-permute-done((f32[4,4,36,128]{3,1,2,0:T(4,128)S(1)}, f32[4,4,36,128]{3,1,2,0:T(4,128)S(1)}, u32[]{:S(2)}, u32[]{:S(2)}) %collective-permute-start) | collective-permute-done | bytes 294944 | tf_op jit(solution)/shard_map/ppermute | solution.py:61
  54.5 0.2 fusion.9
  54.7 0.2 fusion.47
  55.0 4.3 %collective-permute-start.1 = (f32[4,36,128]{2,0,1:T(4,128)S(1)}, f32[4,36,128]{2,0,1:T(4,128)S(1)}, u32[]{:S(2)}, u32[]{:S(2)}) collective-permute-start(f32[4,36,128]{2,0,1:T(4,128)S(1)} %bitcast.66), channel_id=1, source_target_pairs={{0,64},{64,128},{128,192},{192,256},{256,320},{320,384},{384,448},... | collective-permute-start | bytes 221192 | tf_op jit(solution)/shard_map/ppermute | solution.py:52
  59.3 15.9 %collective-permute-start.2 = (f32[4,36,128]{2,0,1:T(4,128)S(1)}, f32[4,36,128]{2,0,1:T(4,128)S(1)}, u32[]{:S(2)}, u32[]{:S(2)}) collective-permute-start(f32[4,36,128]{2,0,1:T(4,128)S(1)} %bitcast.67), channel_id=1, source_target_pairs={{0,960},{64,0},{128,64},{192,128},{256,192},{320,256},{384,320},{4... | collective-permute-start | bytes 221192 | tf_op jit(solution)/shard_map/ppermute | solution.py:52
  75.2 1.9 %collective-permute-start.3 = (f32[4,36,128]{2,0,1:T(4,128)S(1)}, f32[4,36,128]{2,0,1:T(4,128)S(1)}, u32[]{:S(2)}, u32[]{:S(2)}) collective-permute-start(f32[4,36,128]{2,0,1:T(4,128)S(1)} %bitcast.68), channel_id=1, source_target_pairs={{0,128},{64,192},{128,256},{192,320},{256,384},{320,448},{384,512}... | collective-permute-start | bytes 221192 | tf_op jit(solution)/shard_map/ppermute | solution.py:52
  77.1 7.7 %collective-permute-done.3 = f32[4,36,128]{2,0,1:T(4,128)S(1)} collective-permute-done((f32[4,36,128]{2,0,1:T(4,128)S(1)}, f32[4,36,128]{2,0,1:T(4,128)S(1)}, u32[]{:S(2)}, u32[]{:S(2)}) %collective-permute-start.3) | collective-permute-done | bytes 73760 | tf_op jit(solution)/shard_map/ppermute | solution.py:52
  84.9 0.4 copy.64
  85.3 0.7 convolution_bitcast_fusion.1
  86.0 0.7 convolution_bitcast_fusion
  86.8 0.6 copy.74
  87.4 5.1 %all-to-all-start.2 = ((f32[4,36,128]{2,1,0:T(8,128)}), f32[4,36,128]{2,1,0:T(8,128)S(1)}, u32[]{:S(2)}, u32[]{:S(2)}) async-start(f32[4,36,128]{2,1,0:T(8,128)} %copy.74), calls=%async_computation.2 | async-start | bytes 163840 | tf_op jit(solution)/shard_map/all_to_all | solution.py:67
  92.5 0.3 slice_subtract_fusion.1
  92.8 3.8 %fusion.2 = bf16[1,24,32,1024]{3,2,1,0:T(8,128)(2,1)} fusion(f32[1024,128,1]{1,0,2:T(8,128)S(1)} %copy-done.3, f32[24,32,64]{2,1,0:T(8,128)S(1)} %get-tuple-element.21, f32[24,32,64]{2,1,0:T(8,128)S(1)} %get-tuple-element.20), kind=kOutput, calls=%fused_computation.3 | convolution fusion | flops 1209630720 | bytes 2490368 | tf_op jit(solution)/shard_map/cxj,wj->cxw/dot_general | solution.py:112
  96.6 10.2 %all-to-all-done.2 = f32[4,36,128]{2,1,0:T(8,128)S(1)} async-done(((f32[4,36,128]{2,1,0:T(8,128)}), f32[4,36,128]{2,1,0:T(8,128)S(1)}, u32[]{:S(2)}, u32[]{:S(2)}) %all-to-all-start.2) | async-done | bytes 73760 | tf_op jit(solution)/shard_map/all_to_all | solution.py:67
  106.8 0.6 copy.75
  (26 shorter events, 0.6 us)
Async XLA Ops:
  0.6 1.4 %copy-start = (bf16[1,24,32,1024]{3,2,1,0:T(8,128)(2,1)S(1)}, bf16[1,24,32,1024]{3,2,1,0:T(8,128)(2,1)}, u32[]{:S(2)}) copy-start(bf16[1,24,32,1024]{3,2,1,0:T(8,128)(2,1)} %param.4) | copy-start | bytes 4718596
  7.7 33.4 %copy-start.4 = (f32[2,1,24,128]{3,2,1,0:T(8,128)S(1)}, f32[2,1,24,128]{3,2,1,0:T(8,128)}, u32[]{:S(2)}) copy-start(f32[2,1,24,128]{3,2,1,0:T(8,128)} %param.5) | copy-start | bytes 73732
  7.7 33.4 %copy-start.1 = (f32[2,24,24,128]{3,2,1,0:T(8,128)S(1)}, f32[2,24,24,128]{3,2,1,0:T(8,128)}, u32[]{:S(2)}) copy-start(f32[2,24,24,128]{3,2,1,0:T(8,128)} %param.6) | copy-start | bytes 1769476
  42.5 6.1 %copy-start.2 = (f32[2,24,24,64]{3,2,1,0:T(8,128)S(1)}, f32[2,24,24,64]{3,2,1,0:T(8,128)}, u32[]{:S(2)}) copy-start(f32[2,24,24,64]{3,2,1,0:T(8,128)} %get-tuple-element.28) | copy-start | bytes 884740
  43.6 41.2 %all-to-all-start.1 = ((f32[32,2,24,128]{3,1,2,0:T(2,128)}), f32[32,2,24,128]{3,1,2,0:T(2,128)S(1)}, u32[]{:S(2)}, u32[]{:S(2)}) async-start(f32[32,2,24,128]{3,1,2,0:T(2,128)} %broadcast_in_dim.4), calls=%async_computation.1 | async-start | bytes 1572864 | tf_op jit(solution)/shard_map/all_to_all | solution.py:96
  50.9 3.5 %collective-permute-start = (f32[4,4,36,128]{3,1,2,0:T(4,128)S(1)}, f32[4,4,36,128]{3,1,2,0:T(4,128)S(1)}, u32[]{:S(2)}, u32[]{:S(2)}) collective-permute-start(f32[4,4,36,128]{3,1,2,0:T(4,128)S(1)} %bitcast.64), channel_id=1, source_target_pairs={{0,32},{32,0},{1,33},{33,1},{2,34},{34,2},{3,35},{35,3},{4,36},{36... | collective-permute-start | bytes 884744 | tf_op jit(solution)/shard_map/ppermute | solution.py:61
  55.0 22.1 %collective-permute-start.1 = (f32[4,36,128]{2,0,1:T(4,128)S(1)}, f32[4,36,128]{2,0,1:T(4,128)S(1)}, u32[]{:S(2)}, u32[]{:S(2)}) collective-permute-start(f32[4,36,128]{2,0,1:T(4,128)S(1)} %bitcast.66), channel_id=1, source_target_pairs={{0,64},{64,128},{128,192},{192,256},{256,320},{320,384},{384,448},... | collective-permute-start | bytes 221192 | tf_op jit(solution)/shard_map/ppermute | solution.py:52
  59.3 17.8 %collective-permute-start.2 = (f32[4,36,128]{2,0,1:T(4,128)S(1)}, f32[4,36,128]{2,0,1:T(4,128)S(1)}, u32[]{:S(2)}, u32[]{:S(2)}) collective-permute-start(f32[4,36,128]{2,0,1:T(4,128)S(1)} %bitcast.67), channel_id=1, source_target_pairs={{0,960},{64,0},{128,64},{192,128},{256,192},{320,256},{384,320},{4... | collective-permute-start | bytes 221192 | tf_op jit(solution)/shard_map/ppermute | solution.py:52
  75.2 9.6 %collective-permute-start.3 = (f32[4,36,128]{2,0,1:T(4,128)S(1)}, f32[4,36,128]{2,0,1:T(4,128)S(1)}, u32[]{:S(2)}, u32[]{:S(2)}) collective-permute-start(f32[4,36,128]{2,0,1:T(4,128)S(1)} %bitcast.68), channel_id=1, source_target_pairs={{0,128},{64,192},{128,256},{192,320},{256,384},{320,448},{384,512}... | collective-permute-start | bytes 221192 | tf_op jit(solution)/shard_map/ppermute | solution.py:52
  86.8 6.0 %copy-start.3 = (f32[1024,128,1]{1,0,2:T(8,128)S(1)}, f32[1024,128,1]{1,0,2:T(8,128)}, u32[]{:S(2)}) copy-start(f32[1024,128,1]{1,0,2:T(8,128)} %constant.60) | copy-start | bytes 1572868
  87.4 19.3 %all-to-all-start.2 = ((f32[4,36,128]{2,1,0:T(8,128)}), f32[4,36,128]{2,1,0:T(8,128)S(1)}, u32[]{:S(2)}, u32[]{:S(2)}) async-start(f32[4,36,128]{2,1,0:T(8,128)} %copy.74), calls=%async_computation.2 | async-start | bytes 163840 | tf_op jit(solution)/shard_map/all_to_all | solution.py:67

commit v4 on v3

v4 whole, which is shorter than its diff:
```python
import functools
import math

import jax
import jax.numpy as jnp
import ml_dtypes
import numpy as np
from jax import lax
from jax.experimental import pallas as pl
from jax.experimental.pallas import tpu as pltpu
from jax.sharding import Mesh
from jax.sharding import PartitionSpec as P

DP = ("far", "near", "core")
FAR = 4
VMEM = pl.BlockSpec(memory_space=pltpu.VMEM)
SMEM = pl.BlockSpec(memory_space=pltpu.SMEM)
PARAMS = pltpu.CompilerParams(vmem_limit_bytes=24 << 20)


def halves(table):
    high = table.astype(ml_dtypes.bfloat16)
    low = (table - high.astype(np.float64)).astype(ml_dtypes.bfloat16)
    return high, low


def column_table(col_count, modes_y):
    phase = np.arange(col_count)[:, None] * np.arange(modes_y)[None, :] % col_count
    angles = phase * (2.0 * math.pi / col_count)
    return np.concatenate([np.cos(angles), -np.sin(angles)], axis=1)


def row_tables(modes_x, row_count, height):
    phase = np.arange(modes_x)[:, None] * np.arange(height)[None, :] % height
    angles = phase * (2.0 * math.pi / height)
    angles = angles.reshape(modes_x, height // row_count, row_count).transpose(1, 0, 2)
    return np.cos(angles), np.sin(angles)


def split(x):
    high = x.astype(jnp.bfloat16)
    return high, (x - high.astype(jnp.float32)).astype(jnp.bfloat16)


def dot(a, b):
    return jnp.dot(a, b, preferred_element_type=jnp.float32)


def first_half(x, modes_y):
    return lax.broadcasted_iota(jnp.int32, x.shape, x.ndim - 1) < modes_y


def mix(rows, spec, turned):
    high, low = zip(*map(split, spec))
    turned_high, turned_low = zip(*map(split, turned))

    def operand(c):
        return jnp.concatenate(
            [high[c], turned_high[c], low[c], turned_low[c], high[c], turned_high[c]], axis=0
        )

    out, width = [], spec[0].shape[1]
    for c in range(0, len(spec), 2):
        pair = dot(rows, jnp.concatenate([operand(c), operand(c + 1)], axis=1))
        out += [pair[:, :width], pair[:, width:]]
    return out


def forward_kernel(cot_ref, basis_ref, rows_ref, out_ref):
    channels, row_count, col_count = cot_ref.shape
    width = out_ref.shape[2]
    both = dot(cot_ref[...].reshape(channels * row_count, col_count), basis_ref[...])
    col_spec = both[:, :width] + both[:, width:]
    turned = pltpu.roll(col_spec, width // 2, 1)
    turned = jnp.where(first_half(turned, width // 2), turned, -turned)
    parts = [slice(c * row_count, (c + 1) * row_count) for c in range(channels)]
    for c, out in enumerate(mix(rows_ref[...], [col_spec[p] for p in parts], [turned[p] for p in parts])):
        out_ref[:, c, :] = out


def forward(cotangent, block, modes_x, modes_y, height):
    channels, row_count, col_count = cotangent.shape
    basis = np.concatenate(halves(column_table(col_count, modes_y)), axis=1)
    table = np.concatenate(row_tables(modes_x, row_count, height), axis=2) / math.sqrt(height * col_count)
    high, low = halves(table)
    rows = np.concatenate([high, high, low], axis=2)
    rows = lax.dynamic_index_in_dim(jnp.asarray(rows), block, 0, keepdims=False)
    return pl.pallas_call(
        forward_kernel,
        out_shape=jax.ShapeDtypeStruct((modes_x, channels, 2 * modes_y), jnp.float32),
        in_specs=[VMEM, VMEM, VMEM],
        out_specs=VMEM,
        compiler_params=PARAMS,
        name="rows_to_modes",
    )(cotangent, jnp.asarray(basis), rows)


def inverse_kernel(spec_ref, rows_ref, basis_ref, out_ref):
    step, width = out_ref.shape[0], spec_ref.shape[2]
    first = pl.program_id(0) * step
    spec = [spec_ref[first + c] for c in range(step)]
    turned = [pltpu.roll(s, width // 2, 1) for s in spec]
    turned = [jnp.where(first_half(t, width // 2), -t, t) for t in turned]
    high, low = split(jnp.concatenate(mix(rows_ref[...], spec, turned), axis=0))
    raster = dot(jnp.concatenate([high, low, high], axis=1), basis_ref[...])
    out_ref[...] = raster.astype(out_ref.dtype).reshape(out_ref.shape)


def inverse(all_spec, block, row_count, col_count, height):
    channels, modes_x, width = all_spec.shape
    modes_y = width // 2
    high, low = halves(column_table(col_count, modes_y).T)
    basis = np.concatenate([high, high, low], axis=0)
    table = np.concatenate(row_tables(modes_x, row_count, height), axis=1) / math.sqrt(modes_x * modes_y)
    high, low = halves(table.transpose(0, 2, 1))
    rows = np.concatenate([high, high, low], axis=2)
    rows = lax.dynamic_index_in_dim(jnp.asarray(rows), block, 0, keepdims=False)
    step = 8
    return pl.pallas_call(
        inverse_kernel,
        grid=(channels // step,),
        out_shape=jax.ShapeDtypeStruct((channels, row_count, col_count), jnp.bfloat16),
        in_specs=[VMEM, VMEM, VMEM],
        out_specs=pl.BlockSpec((step, row_count, col_count), lambda i: (i, 0, 0)),
        compiler_params=PARAMS,
        name="modes_to_rows",
    )(all_spec, rows, jnp.asarray(basis))


def middle_kernel(got_ref, weights_ref, spectrum_ref, spec_ref, mine_ref, other_ref, one_ref, terms_ref):
    modes, channels, width = spectrum_ref.shape
    sources, near = spec_ref.shape[0], mine_ref.shape[0]
    half = width // 2
    here, core = lax.axis_index("near"), lax.axis_index("core")
    grad = got_ref[pl.ds(0, modes)]
    for s in range(1, sources):
        grad = grad + got_ref[pl.ds(s * modes, modes)]
    turned = pltpu.roll(grad, half, 2)

    for k in range(modes):
        straight, crossed = [], []
        for c in range(channels):
            weight = weights_ref[k, c]
            straight.append(jnp.sum(weight * grad[k], axis=0, keepdims=True))
            crossed.append(jnp.sum(weight * turned[k], axis=0, keepdims=True))
        straight = jnp.concatenate(straight, axis=0)
        crossed = jnp.concatenate(crossed, axis=0)
        left = first_half(straight, half)
        real_part = straight + pltpu.roll(straight, half, 1)
        imag_part = pltpu.roll(crossed, half, 1) - crossed
        one_ref[pl.ds(k, channels, stride=modes), :] = jnp.where(left, real_part, imag_part)
    one = one_ref[...]
    for s in range(sources):
        spec_ref[s] = one

    for k in range(modes):
        own = spectrum_ref[k]
        left = first_half(own, half)
        flipped = pltpu.roll(own, half, 1)
        own_re = jnp.where(left, own, flipped)
        own_im = jnp.where(left, flipped, -own)
        for c in range(channels):
            terms_ref[k, c * channels : (c + 1) * channels] = (
                own_re[c : c + 1] * grad[k] + own_im[c : c + 1] * turned[k]
            )
    rows = mine_ref.shape[1] // FAR
    pairs = rows // modes
    for far in range(FAR):
        for chip in range(near):
            ahead = lax.rem(chip - here + near, near)
            first = 2 * (far * near + chip) * pairs
            for k in range(modes):
                zero = terms_ref[k, first : first + pairs]
                one = terms_ref[k, first + pairs : first + 2 * pairs]
                to = slice(far * rows + k * pairs, far * rows + (k + 1) * pairs)
                mine_ref[ahead, to] = jnp.where(core == 0, zero, one)
                other_ref[ahead, to] = jnp.where(core == 0, one, zero)


def middle(got, weights, spectrum):
    modes, channels, width = spectrum.shape
    sources, near = got.shape[0] // modes, lax.axis_size("near")
    owners = channels * channels * modes // (2 * near)
    terms = jax.ShapeDtypeStruct((near, owners, width), jnp.float32)
    return pl.pallas_call(
        middle_kernel,
        out_shape=(jax.ShapeDtypeStruct((sources, channels * modes, width), jnp.float32), terms, terms),
        in_specs=[VMEM, VMEM, VMEM],
        out_specs=(VMEM, VMEM, VMEM),
        scratch_shapes=[
            pltpu.VMEM((channels * modes, width), jnp.float32),
            pltpu.VMEM((modes, channels * channels, width), jnp.float32),
        ],
        compiler_params=PARAMS,
        name="modes",
    )(got, weights, spectrum)


def shift_near(x, hop):
    near, far = lax.axis_size("near"), lax.axis_size("far")
    chips = near * far
    return lax.ppermute(x, ("far", "near"), [(z, (z + hop) % chips) for z in range(chips)])


def sum_to_owners(mine, other, later):
    far = lax.axis_size("far")
    mine = mine + lax.ppermute(other, "core", [(0, 1), (1, 0)])
    total = mine[0]
    for ahead, hop in ((1, 1), (mine.shape[0] - 1, -1), (2, 2)):
        total = total + shift_near(mine[ahead], hop)
    total, _ = lax.optimization_barrier((total, later))
    total = total.reshape(far, -1, total.shape[1])
    return jnp.sum(lax.all_to_all(total, "far", 0, 0, tiled=True), axis=0)


def body(cotangent, spectrum, weights):
    space_count = lax.axis_size("space")
    _, channels, row_count, col_count = cotangent.shape
    local_modes, modes_y = spectrum.shape[0], spectrum.shape[3] // 2
    height, modes_x = row_count * space_count, local_modes * space_count
    block = lax.axis_index("space")

    partial = forward(cotangent[0], block, modes_x, modes_y, height)
    partial = lax.all_to_all(partial, "space", 0, 0, tiled=True)
    everyone, mine, other = middle(partial, weights, spectrum[:, 0])
    all_spec = lax.all_to_all(everyone, "space", 0, 0, tiled=True)
    grad_weights = sum_to_owners(mine, other, all_spec).reshape(local_modes, -1, 2 * modes_y)

    all_spec = all_spec.reshape(space_count, channels, local_modes, 2 * modes_y).transpose(1, 0, 2, 3)
    all_spec = all_spec.reshape(channels, modes_x, 2 * modes_y)
    grad_input = inverse(all_spec, block, row_count, col_count, height)
    return (grad_input[None], grad_weights)


def solution(mesh):
    dp_count, space_count = mesh.devices.shape
    chips = mesh.devices.reshape(FAR, dp_count // (2 * FAR), 2, space_count)
    return jax.shard_map(
        body,
        mesh=Mesh(chips, DP + ("space",)),
        in_specs=(P(DP, None, "space", None), P("space", DP, None, None), P("space", None, None, None)),
        out_specs=(P(DP, None, "space", None), P("space", DP, None)),
        check_vma=False,
    )
```

time: 108 us -> 102 us (0.944)
  matrix products: 9.61 us -> 0 us
  starting transfers between devices: 34 us -> 41.6 us
  Pallas kernels: 0 us -> 5.34 us
  waiting for transfers between devices: 19.4 us -> 14.7 us
  other arithmetic: 3.54 us -> 0.08 us
    dot_general x6 -> x0, matrix products: 9.61 us -> none  [the longest x1 3.79 us: body(): jnp.einsum('cxj,wj->cxw', back, basis, precision=HP) * inverse_scale]
    all_to_all x1, starting transfers between devices: 5.11 us -> 12.5 us  [sum_to_owners(): return jnp.sum(lax.all_to_all(total, 'far', 0, 0, tiled=True), axis=0)]
    pallas_call x0 -> x3, Pallas kernels: none -> 5.34 us  [the longest x1 2.94 us: inverse(): pl.pallas_call(inverse_kernel, grid=(channels // step,), out_shape=jax.Sh...]
    ppermute x3, waiting for transfers between devices: 7.67 us -> 3.06 us  [shift_near(): lax.ppermute(x, ('far', 'near'), [(z, (z + hop) % chips) for z in range(c...]
    add x4 -> x1, other arithmetic: 1.88 us -> 0.02 us  [sum_to_owners(): total = total + shift_near(mine[ahead], hop)]
    squeeze x0 -> x3, local copies, waits for them, and re-layouts: none -> 1.52 us  [the longest x1 0.77 us: forward(): rows = lax.dynamic_index_in_dim(jnp.asarray(rows), block, 0, keepdims=False)]
    broadcast_in_dim x1 -> x0, local copies, waits for them, and re-layouts: 1.08 us -> none  [body(): jnp.broadcast_to(input_spec[None], (space_count,) + input_spec.shape)]
  transfers between devices with their start and end apart: 6 -> 6, of which waited for: 3 -> 3; matrix products, arithmetic and copies ran while one was open for 7% -> 1% of each run, Pallas kernels for 0% -> 3%
where the time goes in v4:
time: 102 us; the launch traced here: 101 us
  starting transfers between devices  41.6 us (41%)
  blocking collectives  33.1 us (32%)
  waiting for transfers between devices  14.7 us (14%)
  local copies, waits for them, and re-layouts  5.66 us (6%)
  Pallas kernels  5.34 us (5%)
    all_to_all x1, blocking collectives, body(): partial = lax.all_to_all(partial, 'space', 0, 0, tiled=True)  33.1 us
    ppermute x3, starting transfers between devices, shift_near(): lax.ppermute(x, ('far', 'near'), [(z, (z + hop) % chips) for z in range(c...  22.2 us
    all_to_all x1, starting transfers between devices, sum_to_owners(): return jnp.sum(lax.all_to_all(total, 'far', 0, 0, tiled=True), axis=0)  12.5 us
    all_to_all x1, waiting for transfers between devices, sum_to_owners(): return jnp.sum(lax.all_to_all(total, 'far', 0, 0, tiled=True), axis=0)  10.1 us
    all_to_all x1, starting transfers between devices, body(): all_spec = lax.all_to_all(everyone, 'space', 0, 0, tiled=True)  4.92 us
    unnamed x11, local copies, waits for them, and re-layouts  3.08 us
    ppermute x3, waiting for transfers between devices, shift_near(): lax.ppermute(x, ('far', 'near'), [(z, (z + hop) % chips) for z in range(c...  3.06 us
    pallas_call x1, Pallas kernels, inverse(): pl.pallas_call(inverse_kernel, grid=(channels // step,), out_shape=jax.Sh...  2.94 us
  transfers between devices with their start and end apart: 6, of which 3 were waited for; matrix products, arithmetic and copies ran while one was open for 1% of the time, Pallas kernels for 3%

profile of v4, /device:TPU:8, one launch (start us, length us, event | category | flops | bytes accessed | tf_op | source)
XLA Modules:
  0.0 101.3 jit_solution(17411220043511048905)
XLA Ops:
  0.6 0.8 dynamic-slice_bitcast_fusion.rows_ref
  1.4 0.0 copy-start
  1.4 1.4 %copy-done = bf16[1,24,32,1024]{3,2,1,0:T(8,128)(2,1)S(1)} copy-done((bf16[1,24,32,1024]{3,2,1,0:T(8,128)(2,1)S(1)}, bf16[1,24,32,1024]{3,2,1,0:T(8,128)(2,1)}, u32[]{:S(2)}) %copy-start) | copy-done | bytes 1572888
  2.8 0.0 copy-start.3
  2.8 1.0 %copy-done.3 = bf16[1024,256]{1,0:T(8,128)(2,1)S(1)} copy-done((bf16[1024,256]{1,0:T(8,128)(2,1)S(1)}, bf16[1024,256]{1,0:T(8,128)(2,1)}, u32[]{:S(2)}) %copy-start.3) | copy-done | bytes 524312
  3.9 0.0 copy-start.2
  3.9 0.0 copy-start.4
  3.9 1.2 %rows_to_modes.1 = f32[64,24,128]{2,1,0:T(8,128)S(1)} custom-call(bf16[24,32,1024]{2,1,0:T(8,128)(2,1)S(1)} %bitcast.26, bf16[1024,256]{1,0:T(8,128)(2,1)S(1)} %copy-done.3, bf16[64,192]{1,0:T(8,128)(2,1)S(1)} %dynamic-slice_bitcast_fusion.rows_ref), custom_call_target="tpu_custom_call" | custom-call | tf_op jit(solution)/shard_map/rows_to_modes/pallas_call | solution.py:88
  5.0 33.1 %all_to_all.15.got_ref = f32[64,24,128]{2,1,0:T(8,128)S(1)} all-to-all(f32[64,24,128]{2,1,0:T(8,128)S(1)} %rows_to_modes.1), channel_id=1, replica_groups=mesh['far'=4,'near'=4,'core'=2,'space'=32] {'space'}, dimensions={0} | all-to-all | bytes 1572864 | tf_op jit(solution)/shard_map/all_to_all | solution.py:224
  38.2 0.0 copy-done.2
  38.2 0.0 copy-done.4
  38.2 1.2 %modes.1 = (f32[32,48,128]{2,1,0:T(8,128)}, f32[4,144,128]{2,1,0:T(8,128)S(1)}, f32[4,144,128]{2,1,0:T(8,128)S(1)}) custom-call(f32[64,24,128]{2,1,0:T(8,128)S(1)} %all_to_all.15.got_ref, f32[2,24,24,128]{3,2,1,0:T(8,128)S(1)} %copy-done.2, f32[2,24,128]{2,1,0:T(8,128)S(1)} %bitcast.27), custom_call_target="tpu_custom_call" | custom-call | tf_op jit(solution)/shard_map/modes/pallas_call | solution.py:185
  39.4 4.9 %all-to-all-start.1 = ((f32[32,48,128]{2,1,0:T(8,128)}), f32[32,48,128]{2,1,0:T(8,128)S(1)}, u32[]{:S(2)}, u32[]{:S(2)}) async-start(f32[32,48,128]{2,1,0:T(8,128)} %get-tuple-element.6), calls=%async_computation.1 | async-start | bytes 1572864 | tf_op jit(solution)/shard_map/all_to_all | solution.py:226
  44.3 1.9 %collective-permute-start = (f32[4,144,128]{2,1,0:T(8,128)S(1)}, f32[4,144,128]{2,1,0:T(8,128)S(1)}, u32[]{:S(2)}, u32[]{:S(2)}) collective-permute-start(f32[4,144,128]{2,1,0:T(8,128)S(1)} %get-tuple-element.8), channel_id=1, source_target_pairs={{0,32},{32,0},{1,33},{33,1},{2,34},{34,2},{3,35},{35,3},{4,36},{36... | collective-permute-start | bytes 884744 | tf_op jit(solution)/shard_map/ppermute | solution.py:207
  46.3 1.5 %collective-permute-done = f32[4,144,128]{2,1,0:T(8,128)S(1)} collective-permute-done((f32[4,144,128]{2,1,0:T(8,128)S(1)}, f32[4,144,128]{2,1,0:T(8,128)S(1)}, u32[]{:S(2)}, u32[]{:S(2)}) %collective-permute-start) | collective-permute-done | bytes 294944 | tf_op jit(solution)/shard_map/ppermute | solution.py:207
  47.9 0.0 copy-start.1
  47.9 4.4 %collective-permute-start.1 = (f32[144,128]{1,0:T(8,128)S(1)}, f32[144,128]{1,0:T(8,128)S(1)}, u32[]{:S(2)}, u32[]{:S(2)}) collective-permute-start(f32[144,128]{1,0:T(8,128)S(1)} %get-tuple-element.12), channel_id=1, source_target_pairs={{0,64},{64,128},{128,192},{192,256},{256,320},{320,384},{384,448},... | collective-permute-start | bytes 221192 | tf_op jit(solution)/shard_map/ppermute | solution.py:202
  52.3 6.1 %collective-permute-start.3 = (f32[144,128]{1,0:T(8,128)S(1)}, f32[144,128]{1,0:T(8,128)S(1)}, u32[]{:S(2)}, u32[]{:S(2)}) collective-permute-start(f32[144,128]{1,0:T(8,128)S(1)} %get-tuple-element.13), channel_id=1, source_target_pairs={{0,128},{64,192},{128,256},{192,320},{256,384},{320,448},{384,512}... | collective-permute-start | bytes 221192 | tf_op jit(solution)/shard_map/ppermute | solution.py:202
  58.4 11.7 %collective-permute-start.2 = (f32[144,128]{1,0:T(8,128)S(1)}, f32[144,128]{1,0:T(8,128)S(1)}, u32[]{:S(2)}, u32[]{:S(2)}) collective-permute-start(f32[144,128]{1,0:T(8,128)S(1)} %get-tuple-element.14), channel_id=1, source_target_pairs={{0,960},{64,0},{128,64},{192,128},{256,192},{320,256},{384,320},{4... | collective-permute-start | bytes 221192 | tf_op jit(solution)/shard_map/ppermute | solution.py:202
  70.1 0.0 collective-permute-done.1
  70.1 3.1 %collective-permute-done.3 = f32[144,128]{1,0:T(8,128)S(1)} collective-permute-done((f32[144,128]{1,0:T(8,128)S(1)}, f32[144,128]{1,0:T(8,128)S(1)}, u32[]{:S(2)}, u32[]{:S(2)}) %collective-permute-start.3) | collective-permute-done | bytes 73760 | tf_op jit(solution)/shard_map/ppermute | solution.py:202
  73.2 0.0 collective-permute-done.2
  73.2 0.0 all-to-all-done.1
  73.2 0.6 reshape.18
  73.9 12.5 %all-to-all-start.2 = ((f32[4,36,128]{2,1,0:T(8,128)}), f32[4,36,128]{2,1,0:T(8,128)S(1)}, u32[]{:S(2)}, u32[]{:S(2)}) async-start(f32[4,36,128]{2,1,0:T(8,128)} %reshape.18), calls=%async_computation.2 | async-start | bytes 163840 | tf_op jit(solution)/shard_map/all_to_all | solution.py:213
  86.4 0.7 dynamic-slice_bitcast_fusion.1.rows_ref
  87.1 0.4 copy.10
  87.5 0.0 copy-done.1
  87.6 2.9 %modes_to_rows.1 = bf16[24,32,1024]{2,1,0:T(8,128)(2,1)} custom-call(f32[24,64,128]{2,1,0:T(8,128)S(1)} %bitcast.25, bf16[32,384]{1,0:T(8,128)(2,1)S(1)} %dynamic-slice_bitcast_fusion.1.rows_ref, bf16[384,1024]{1,0:T(8,128)(2,1)S(1)} %copy-done.1), custom_call_target="tpu_custom_call" | custom-call | tf_op jit(solution)/shard_map/modes_to_rows/pallas_call | solution.py:119
  90.5 10.1 %all-to-all-done.2 = f32[4,36,128]{2,1,0:T(8,128)S(1)} async-done(((f32[4,36,128]{2,1,0:T(8,128)}), f32[4,36,128]{2,1,0:T(8,128)S(1)}, u32[]{:S(2)}, u32[]{:S(2)}) %all-to-all-start.2) | async-done | bytes 73760 | tf_op jit(solution)/shard_map/all_to_all | solution.py:213
  100.6 0.6 copy.11
  (5 shorter events, 0.1 us)
Async XLA Ops:
  1.4 1.4 %copy-start = (bf16[1,24,32,1024]{3,2,1,0:T(8,128)(2,1)S(1)}, bf16[1,24,32,1024]{3,2,1,0:T(8,128)(2,1)}, u32[]{:S(2)}) copy-start(bf16[1,24,32,1024]{3,2,1,0:T(8,128)(2,1)} %param.7) | copy-start | bytes 4718596
  2.8 1.0 %copy-start.3 = (bf16[1024,256]{1,0:T(8,128)(2,1)S(1)}, bf16[1024,256]{1,0:T(8,128)(2,1)}, u32[]{:S(2)}) copy-start(bf16[1024,256]{1,0:T(8,128)(2,1)} %constant.25.clone.basis_ref) | copy-start | bytes 1572868
  3.9 34.3 %copy-start.2 = (f32[2,24,24,128]{3,2,1,0:T(8,128)S(1)}, f32[2,24,24,128]{3,2,1,0:T(8,128)}, u32[]{:S(2)}) copy-start(f32[2,24,24,128]{3,2,1,0:T(8,128)} %weights_ref.1) | copy-start | bytes 1769476
  3.9 34.3 %copy-start.4 = (f32[2,1,24,128]{3,2,1,0:T(8,128)S(1)}, f32[2,1,24,128]{3,2,1,0:T(8,128)}, u32[]{:S(2)}) copy-start(f32[2,1,24,128]{3,2,1,0:T(8,128)} %param.8) | copy-start | bytes 73732
  39.4 33.8 %all-to-all-start.1 = ((f32[32,48,128]{2,1,0:T(8,128)}), f32[32,48,128]{2,1,0:T(8,128)S(1)}, u32[]{:S(2)}, u32[]{:S(2)}) async-start(f32[32,48,128]{2,1,0:T(8,128)} %get-tuple-element.6), calls=%async_computation.1 | async-start | bytes 1572864 | tf_op jit(solution)/shard_map/all_to_all | solution.py:226
  44.3 3.5 %collective-permute-start = (f32[4,144,128]{2,1,0:T(8,128)S(1)}, f32[4,144,128]{2,1,0:T(8,128)S(1)}, u32[]{:S(2)}, u32[]{:S(2)}) collective-permute-start(f32[4,144,128]{2,1,0:T(8,128)S(1)} %get-tuple-element.8), channel_id=1, source_target_pairs={{0,32},{32,0},{1,33},{33,1},{2,34},{34,2},{3,35},{35,3},{4,36},{36... | collective-permute-start | bytes 884744 | tf_op jit(solution)/shard_map/ppermute | solution.py:207
  47.9 39.7 %copy-start.1 = (bf16[384,1024]{1,0:T(8,128)(2,1)S(1)}, bf16[384,1024]{1,0:T(8,128)(2,1)}, u32[]{:S(2)}) copy-start(bf16[384,1024]{1,0:T(8,128)(2,1)} %constant.27.clone.basis_ref) | copy-start | bytes 2359300
  47.9 22.2 %collective-permute-start.1 = (f32[144,128]{1,0:T(8,128)S(1)}, f32[144,128]{1,0:T(8,128)S(1)}, u32[]{:S(2)}, u32[]{:S(2)}) collective-permute-start(f32[144,128]{1,0:T(8,128)S(1)} %get-tuple-element.12), channel_id=1, source_target_pairs={{0,64},{64,128},{128,192},{192,256},{256,320},{320,384},{384,448},... | collective-permute-start | bytes 221192 | tf_op jit(solution)/shard_map/ppermute | solution.py:202
  52.3 20.9 %collective-permute-start.3 = (f32[144,128]{1,0:T(8,128)S(1)}, f32[144,128]{1,0:T(8,128)S(1)}, u32[]{:S(2)}, u32[]{:S(2)}) collective-permute-start(f32[144,128]{1,0:T(8,128)S(1)} %get-tuple-element.13), channel_id=1, source_target_pairs={{0,128},{64,192},{128,256},{192,320},{256,384},{320,448},{384,512}... | collective-permute-start | bytes 221192 | tf_op jit(solution)/shard_map/ppermute | solution.py:202
  58.4 14.8 %collective-permute-start.2 = (f32[144,128]{1,0:T(8,128)S(1)}, f32[144,128]{1,0:T(8,128)S(1)}, u32[]{:S(2)}, u32[]{:S(2)}) collective-permute-start(f32[144,128]{1,0:T(8,128)S(1)} %get-tuple-element.14), channel_id=1, source_target_pairs={{0,960},{64,0},{128,64},{192,128},{256,192},{320,256},{384,320},{4... | collective-permute-start | bytes 221192 | tf_op jit(solution)/shard_map/ppermute | solution.py:202
  73.9 26.8 %all-to-all-start.2 = ((f32[4,36,128]{2,1,0:T(8,128)}), f32[4,36,128]{2,1,0:T(8,128)S(1)}, u32[]{:S(2)}, u32[]{:S(2)}) async-start(f32[4,36,128]{2,1,0:T(8,128)} %reshape.18), calls=%async_computation.2 | async-start | bytes 163840 | tf_op jit(solution)/shard_map/all_to_all | solution.py:213

commit v5 on v4

--- a/solution.py
+++ b/solution.py
@@ -12,9 +12,12 @@
 from jax.sharding import PartitionSpec as P
 
 DP = ("far", "near", "core")
+SPACE = ("row", "column")
 FAR = 4
+ROWS = 4
+HOPS = (0, 1, 2, -1)
 VMEM = pl.BlockSpec(memory_space=pltpu.VMEM)
-SMEM = pl.BlockSpec(memory_space=pltpu.SMEM)
+HBM = pl.BlockSpec(memory_space=pltpu.HBM)
 PARAMS = pltpu.CompilerParams(vmem_limit_bytes=24 << 20)
 
 
@@ -66,33 +69,57 @@
     return out
 
 
-def forward_kernel(cot_ref, basis_ref, rows_ref, out_ref):
+def forward_kernel(cot_hbm, basis_hbm, rows_hbm, out_ref, cot_ref, basis_ref, rows_ref, sems):
     channels, row_count, col_count = cot_ref.shape
-    width = out_ref.shape[2]
-    both = dot(cot_ref[...].reshape(channels * row_count, col_count), basis_ref[...])
-    col_spec = both[:, :width] + both[:, width:]
-    turned = pltpu.roll(col_spec, width // 2, 1)
-    turned = jnp.where(first_half(turned, width // 2), turned, -turned)
-    parts = [slice(c * row_count, (c + 1) * row_count) for c in range(channels)]
-    for c, out in enumerate(mix(rows_ref[...], [col_spec[p] for p in parts], [turned[p] for p in parts])):
-        out_ref[:, c, :] = out
-
-
-def forward(cotangent, block, modes_x, modes_y, height):
+    width, chunks = out_ref.shape[2], sems.shape[0] - 2
+    step = channels // chunks
+    copies = [
+        pltpu.make_async_copy(basis_hbm, basis_ref, sems.at[chunks]),
+        pltpu.make_async_copy(rows_hbm.at[lax.axis_index(SPACE)], rows_ref, sems.at[chunks + 1]),
+    ]
+    pieces = [slice(i * step, (i + 1) * step) for i in range(chunks)]
+    loads = [
+        pltpu.make_async_copy(cot_hbm.at[piece], cot_ref.at[piece], sems.at[i])
+        for i, piece in enumerate(pieces)
+    ]
+    loads[0].start()
+    for copy in copies + loads[1:]:
+        copy.start()
+    for copy in copies:
+        copy.wait()
+    for piece, load in zip(pieces, loads):
+        load.wait()
+        both = dot(cot_ref[piece].reshape(step * row_count, col_count), basis_ref[...])
+        col_spec = both[:, :width] + both[:, width:]
+        turned = pltpu.roll(col_spec, width // 2, 1)
+        turned = jnp.where(first_half(turned, width // 2), turned, -turned)
+        parts = [slice(c * row_count, (c + 1) * row_count) for c in range(step)]
+        mixed = mix(rows_ref[...], [col_spec[p] for p in parts], [turned[p] for p in parts])
+        for c, out in enumerate(mixed):
+            out_ref[:, piece.start + c, :] = out
+
+
+def forward(cotangent, modes_x, modes_y, height):
     channels, row_count, col_count = cotangent.shape
     basis = np.concatenate(halves(column_table(col_count, modes_y)), axis=1)
     table = np.concatenate(row_tables(modes_x, row_count, height), axis=2) / math.sqrt(height * col_count)
     high, low = halves(table)
     rows = np.concatenate([high, high, low], axis=2)
-    rows = lax.dynamic_index_in_dim(jnp.asarray(rows), block, 0, keepdims=False)
+    chunks = 3
     return pl.pallas_call(
         forward_kernel,
         out_shape=jax.ShapeDtypeStruct((modes_x, channels, 2 * modes_y), jnp.float32),
-        in_specs=[VMEM, VMEM, VMEM],
+        in_specs=[HBM, HBM, HBM],
         out_specs=VMEM,
+        scratch_shapes=[
+            pltpu.VMEM(cotangent.shape, jnp.bfloat16),
+            pltpu.VMEM(basis.shape, jnp.bfloat16),
+            pltpu.VMEM(rows.shape[1:], jnp.bfloat16),
+            pltpu.SemaphoreType.DMA((chunks + 2,)),
+        ],
         compiler_params=PARAMS,
         name="rows_to_modes",
-    )(cotangent, jnp.asarray(basis), rows)
+    )(*(pltpu.with_memory_space_constraint(x, pltpu.HBM) for x in (cotangent, jnp.asarray(basis), jnp.asarray(rows))))
 
 
 def inverse_kernel(spec_ref, rows_ref, basis_ref, out_ref):
@@ -129,11 +156,10 @@
 
 def middle_kernel(got_ref, weights_ref, spectrum_ref, spec_ref, mine_ref, other_ref, one_ref, terms_ref):
     modes, channels, width = spectrum_ref.shape
-    sources, near = spec_ref.shape[0], mine_ref.shape[0]
     half = width // 2
     here, core = lax.axis_index("near"), lax.axis_index("core")
     grad = got_ref[pl.ds(0, modes)]
-    for s in range(1, sources):
+    for s in range(1, got_ref.shape[0] // modes):
         grad = grad + got_ref[pl.ds(s * modes, modes)]
     turned = pltpu.roll(grad, half, 2)
 
@@ -150,7 +176,7 @@
         imag_part = pltpu.roll(crossed, half, 1) - crossed
         one_ref[pl.ds(k, channels, stride=modes), :] = jnp.where(left, real_part, imag_part)
     one = one_ref[...]
-    for s in range(sources):
+    for s in range(spec_ref.shape[0]):
         spec_ref[s] = one
 
     for k in range(modes):
@@ -160,71 +186,74 @@
         own_re = jnp.where(left, own, flipped)
         own_im = jnp.where(left, flipped, -own)
         for c in range(channels):
-            terms_ref[k, c * channels : (c + 1) * channels] = (
+            terms_ref[pl.ds(c * channels * modes + k, channels, stride=modes), :] = (
                 own_re[c : c + 1] * grad[k] + own_im[c : c + 1] * turned[k]
             )
-    rows = mine_ref.shape[1] // FAR
-    pairs = rows // modes
-    for far in range(FAR):
-        for chip in range(near):
-            ahead = lax.rem(chip - here + near, near)
-            first = 2 * (far * near + chip) * pairs
-            for k in range(modes):
-                zero = terms_ref[k, first : first + pairs]
-                one = terms_ref[k, first + pairs : first + 2 * pairs]
-                to = slice(far * rows + k * pairs, far * rows + (k + 1) * pairs)
-                mine_ref[ahead, to] = jnp.where(core == 0, zero, one)
-                other_ref[ahead, to] = jnp.where(core == 0, one, zero)
-
-
-def middle(got, weights, spectrum):
+    near, far, rows, _ = mine_ref.shape
+    owned = channels * channels * modes // (2 * near * far)
+    terms_ref[pl.ds(channels * channels * modes, 8), :] = jnp.zeros((8, width), jnp.float32)
+    for ahead in range(near):
+        column = lax.rem(here + HOPS[ahead] + near, near)
+        for target in range(far):
+            first = (target * near + column) * (2 * owned)
+            zero = terms_ref[pl.ds(first, rows), :]
+            one = terms_ref[pl.ds(first + owned, rows), :]
+            mine_ref[ahead, target] = jnp.where(core == 0, zero, one)
+            other_ref[ahead, target] = jnp.where(core == 0, one, zero)
+
+
+def middle(got, weights, spectrum, copies):
     modes, channels, width = spectrum.shape
-    sources, near = got.shape[0] // modes, lax.axis_size("near")
-    owners = channels * channels * modes // (2 * near)
-    terms = jax.ShapeDtypeStruct((near, owners, width), jnp.float32)
+    near = lax.axis_size("near")
+    far = lax.axis_size("far")
+    rows = channels * channels * modes // (2 * near * far)
+    terms = jax.ShapeDtypeStruct((near, far, pl.cdiv(rows, 8) * 8, width), jnp.float32)
     return pl.pallas_call(
         middle_kernel,
-        out_shape=(jax.ShapeDtypeStruct((sources, channels * modes, width), jnp.float32), terms, terms),
+        out_shape=(jax.ShapeDtypeStruct((copies, channels * modes, width), jnp.float32), terms, terms),
         in_specs=[VMEM, VMEM, VMEM],
         out_specs=(VMEM, VMEM, VMEM),
         scratch_shapes=[
             pltpu.VMEM((channels * modes, width), jnp.float32),
-            pltpu.VMEM((modes, channels * channels, width), jnp.float32),
+            pltpu.VMEM((channels * channels * modes + 8, width), jnp.float32),
         ],
         compiler_params=PARAMS,
         name="modes",
     )(got, weights, spectrum)
 
 
-def shift_near(x, hop):
+def shift(x, hop):
     near, far = lax.axis_size("near"), lax.axis_size("far")
     chips = near * far
     return lax.ppermute(x, ("far", "near"), [(z, (z + hop) % chips) for z in range(chips)])
 
 
 def sum_to_owners(mine, other, later):
-    far = lax.axis_size("far")
     mine = mine + lax.ppermute(other, "core", [(0, 1), (1, 0)])
     total = mine[0]
-    for ahead, hop in ((1, 1), (mine.shape[0] - 1, -1), (2, 2)):
-        total = total + shift_near(mine[ahead], hop)
+    for ahead in range(1, mine.shape[0]):
+        total = total + shift(mine[ahead], HOPS[ahead])
     total, _ = lax.optimization_barrier((total, later))
-    total = total.reshape(far, -1, total.shape[1])
-    return jnp.sum(lax.all_to_all(total, "far", 0, 0, tiled=True), axis=0)
+    return lax.all_to_all(total, "far", 0, 0, tiled=True)
 
 
 def body(cotangent, spectrum, weights):
-    space_count = lax.axis_size("space")
+    space_count = lax.axis_size(SPACE)
     _, channels, row_count, col_count = cotangent.shape
     local_modes, modes_y = spectrum.shape[0], spectrum.shape[3] // 2
     height, modes_x = row_count * space_count, local_modes * space_count
-    block = lax.axis_index("space")
-
-    partial = forward(cotangent[0], block, modes_x, modes_y, height)
-    partial = lax.all_to_all(partial, "space", 0, 0, tiled=True)
-    everyone, mine, other = middle(partial, weights, spectrum[:, 0])
-    all_spec = lax.all_to_all(everyone, "space", 0, 0, tiled=True)
-    grad_weights = sum_to_owners(mine, other, all_spec).reshape(local_modes, -1, 2 * modes_y)
+    block = lax.axis_index(SPACE)
+
+    partial = forward(cotangent[0], modes_x, modes_y, height)
+    partial = lax.all_to_all(partial, "row", 0, 0, tiled=True)
+    partial = jnp.sum(partial.reshape((lax.axis_size("row"), -1) + partial.shape[1:]), axis=0)
+    partial = lax.all_to_all(partial, "column", 0, 0, tiled=True)
+    everyone, mine, other = middle(partial, weights, spectrum[:, 0], space_count)
+    all_spec = lax.all_to_all(everyone, SPACE, 0, 0, tiled=True)
+    pairs = channels * channels // lax.axis_size(DP)
+    terms = sum_to_owners(mine, other, all_spec)
+    terms = terms.reshape(terms.shape[0], -1, local_modes, 2 * modes_y)[:, :pairs]
+    grad_weights = jnp.sum(terms, axis=0).transpose(1, 0, 2)
 
     all_spec = all_spec.reshape(space_count, channels, local_modes, 2 * modes_y).transpose(1, 0, 2, 3)
     all_spec = all_spec.reshape(channels, modes_x, 2 * modes_y)
@@ -234,11 +263,11 @@
 
 def solution(mesh):
     dp_count, space_count = mesh.devices.shape
-    chips = mesh.devices.reshape(FAR, dp_count // (2 * FAR), 2, space_count)
+    chips = mesh.devices.reshape(FAR, dp_count // (2 * FAR), 2, ROWS, space_count // ROWS)
     return jax.shard_map(
         body,
-        mesh=Mesh(chips, DP + ("space",)),
-        in_specs=(P(DP, None, "space", None), P("space", DP, None, None), P("space", None, None, None)),
-        out_specs=(P(DP, None, "space", None), P("space", DP, None)),
+        mesh=Mesh(chips, DP + SPACE),
+        in_specs=(P(DP, None, SPACE, None), P(SPACE, DP, None, None), P(SPACE, None, None, None)),
+        out_specs=(P(DP, None, SPACE, None), P(SPACE, DP, None)),
         check_vma=False,
     )

time: 102 us -> 97.8 us (0.959)
  starting transfers between devices: 41.6 us -> 30.7 us
  waiting for transfers between devices: 14.7 us -> 19.7 us
  local copies, waits for them, and re-layouts: 5.66 us -> 1.19 us
  blocking collectives: 33.1 us -> 35.8 us
  Pallas kernels: 5.34 us -> 7.66 us
  other arithmetic: 0.08 us -> 1.38 us
    all_to_all x2, starting transfers between devices: 17.4 us -> 10.2 us  [the longest x1 5.18 us: sum_to_owners(): return lax.all_to_all(total, 'far', 0, 0, tiled=True)]
    ppermute x3, waiting for transfers between devices: 3.06 us -> 8.03 us  [shift(): lax.ppermute(x, ('far', 'near'), [(z, (z + hop) % chips) for z in range(c...]
    ppermute x3, starting transfers between devices: 22.2 us -> 18.5 us  [shift(): lax.ppermute(x, ('far', 'near'), [(z, (z + hop) % chips) for z in range(c...]
    unnamed x11 -> x6, local copies, waits for them, and re-layouts: 3.08 us -> 0.02 us
    all_to_all x1 -> x2, blocking collectives: 33.1 us -> 35.8 us  [the longest x1 19.3 us: body(): partial = lax.all_to_all(partial, 'column', 0, 0, tiled=True)]
    pallas_call x1, Pallas kernels: 1.18 us -> 3.37 us  [forward(): pl.pallas_call(forward_kernel, out_shape=jax.ShapeDtypeStruct((modes_x, c...]
  transfers between devices with their start and end apart: 6 -> 6, of which waited for: 3 -> 4; matrix products, arithmetic and copies ran while one was open for 1% -> 2% of each run, Pallas kernels for 3% -> 3%
where the time goes in v5:
time: 97.8 us; the launch traced here: 97.2 us
  blocking collectives  35.8 us (37%)
  starting transfers between devices  30.7 us (31%)
  waiting for transfers between devices  19.7 us (20%)
  Pallas kernels  7.66 us (8%)
  other arithmetic  1.38 us (1%)
  local copies, waits for them, and re-layouts  1.19 us (1%)
    all_to_all x1, blocking collectives, body(): partial = lax.all_to_all(partial, 'column', 0, 0, tiled=True)  19.3 us
    ppermute x3, starting transfers between devices, shift(): lax.ppermute(x, ('far', 'near'), [(z, (z + hop) % chips) for z in range(c...  18.5 us
    all_to_all x1, blocking collectives, body(): partial = lax.all_to_all(partial, 'row', 0, 0, tiled=True)  16.5 us
    all_to_all x1, waiting for transfers between devices, sum_to_owners(): return lax.all_to_all(total, 'far', 0, 0, tiled=True)  10.1 us
    ppermute x3, waiting for transfers between devices, shift(): lax.ppermute(x, ('far', 'near'), [(z, (z + hop) % chips) for z in range(c...  8.03 us
    all_to_all x1, starting transfers between devices, sum_to_owners(): return lax.all_to_all(total, 'far', 0, 0, tiled=True)  5.18 us
    all_to_all x1, starting transfers between devices, body(): all_spec = lax.all_to_all(everyone, SPACE, 0, 0, tiled=True)  5.02 us
    pallas_call x1, Pallas kernels, forward(): pl.pallas_call(forward_kernel, out_shape=jax.ShapeDtypeStruct((modes_x, c...  3.37 us
  transfers between devices with their start and end apart: 6, of which 4 were waited for; matrix products, arithmetic and copies ran while one was open for 2% of the time, Pallas kernels for 3%

profile of v5, /device:TPU:8, one launch (start us, length us, event | category | flops | bytes accessed | tf_op | source)
XLA Modules:
  0.0 97.2 jit_solution(4994775056041119157)
XLA Ops:
  0.6 3.4 %rows_to_modes.1 = f32[64,24,128]{2,1,0:T(8,128)S(1)} custom-call(bf16[24,32,1024]{2,1,0:T(8,128)(2,1)} %bitcast.31, bf16[1024,256]{1,0:T(8,128)(2,1)} %constant.26.clone.basis_hbm, bf16[32,64,192]{2,1,0:T(8,128)(2,1)} %constant.27.clone.rows_hbm), custom_call_target="tpu_custom_call" | custom-call | tf_op jit(solution)/shard_map/rows_to_modes/pallas_call | solution.py:109
  4.0 0.0 copy-start.1
  4.0 0.0 copy-start.2
  4.0 16.5 %all_to_all.20 = f32[64,24,128]{2,1,0:T(8,128)S(1)} all-to-all(f32[64,24,128]{2,1,0:T(8,128)S(1)} %rows_to_modes.1), channel_id=1, replica_groups=mesh['far'=4,'near'=4,'core'=2,'row'=4,'column'=8] {'row'}, dimensions={0} | all-to-all | bytes 1572864 | tf_op jit(solution)/shard_map/all_to_all | solution.py:248
  20.6 19.3 %all_to_all.21.got_ref = f32[16,24,128]{2,1,0:T(8,128)S(1)} all-to-all(f32[16,24,128]{2,1,0:T(8,128)S(1)} %reduce_sum.18), channel_id=1, replica_groups=mesh['far'=4,'near'=4,'core'=2,'row'=4,'column'=8] {'column'}, dimensions={0} | all-to-all | bytes 393216 | tf_op jit(solution)/shard_map/all_to_all | solution.py:250
  39.9 0.0 copy-done.1
  39.9 0.0 copy-done.2
  39.9 1.3 %modes.1 = (f32[32,48,128]{2,1,0:T(8,128)}, f32[4,4,40,128]{3,2,1,0:T(8,128)S(1)}, f32[4,4,40,128]{3,2,1,0:T(8,128)S(1)}) custom-call(f32[16,24,128]{2,1,0:T(8,128)S(1)} %all_to_all.21.got_ref, f32[2,24,24,128]{3,2,1,0:T(8,128)S(1)} %copy-done.1, f32[2,24,128]{2,1,0:T(8,128)S(1)} %bitcast.27), custom_call_target="tpu_custom_call" | custom-call | tf_op jit(solution)/shard_map/modes/pallas_call | solution.py:211
  41.3 5.0 %all-to-all-start.2 = ((f32[32,48,128]{2,1,0:T(8,128)}), f32[32,48,128]{2,1,0:T(8,128)S(1)}, u32[]{:S(2)}, u32[]{:S(2)}) async-start(f32[32,48,128]{2,1,0:T(8,128)} %get-tuple-element.6), calls=%async_computation.2 | async-start | bytes 1572864 | tf_op jit(solution)/shard_map/all_to_all | solution.py:252
  46.3 1.9 %collective-permute-start = (f32[4,4,40,128]{3,2,1,0:T(8,128)S(1)}, f32[4,4,40,128]{3,2,1,0:T(8,128)S(1)}, u32[]{:S(2)}, u32[]{:S(2)}) collective-permute-start(f32[4,4,40,128]{3,2,1,0:T(8,128)S(1)} %get-tuple-element.8), channel_id=1, source_target_pairs={{0,32},{32,0},{1,33},{33,1},{2,34},{34,2},{3,35},{35,3},{4,36},{36... | collective-permute-start | bytes 983048 | tf_op jit(solution)/shard_map/ppermute | solution.py:232
  48.2 1.6 %collective-permute-done = f32[4,4,40,128]{3,2,1,0:T(8,128)S(1)} collective-permute-done((f32[4,4,40,128]{3,2,1,0:T(8,128)S(1)}, f32[4,4,40,128]{3,2,1,0:T(8,128)S(1)}, u32[]{:S(2)}, u32[]{:S(2)}) %collective-permute-start) | collective-permute-done | bytes 327712 | tf_op jit(solution)/shard_map/ppermute | solution.py:232
  49.8 0.1 add.21
  49.9 0.0 copy-start
  49.9 2.1 %collective-permute-start.1 = (f32[4,40,128]{2,1,0:T(8,128)S(1)}, f32[4,40,128]{2,1,0:T(8,128)S(1)}, u32[]{:S(2)}, u32[]{:S(2)}) collective-permute-start(f32[4,40,128]{2,1,0:T(8,128)S(1)} %get-tuple-element.10), channel_id=1, source_target_pairs={{0,64},{64,128},{128,192},{192,256},{256,320},{320,384},{384,448},... | collective-permute-start | bytes 245768 | tf_op jit(solution)/shard_map/ppermute | solution.py:228
  52.0 14.6 %collective-permute-start.3 = (f32[4,40,128]{2,1,0:T(8,128)S(1)}, f32[4,40,128]{2,1,0:T(8,128)S(1)}, u32[]{:S(2)}, u32[]{:S(2)}) collective-permute-start(f32[4,40,128]{2,1,0:T(8,128)S(1)} %get-tuple-element.11), channel_id=1, source_target_pairs={{0,960},{64,0},{128,64},{192,128},{256,192},{320,256},{384,320},{4... | collective-permute-start | bytes 245768 | tf_op jit(solution)/shard_map/ppermute | solution.py:228
  66.5 1.9 %collective-permute-start.2 = (f32[4,40,128]{2,1,0:T(8,128)S(1)}, f32[4,40,128]{2,1,0:T(8,128)S(1)}, u32[]{:S(2)}, u32[]{:S(2)}) collective-permute-start(f32[4,40,128]{2,1,0:T(8,128)S(1)} %get-tuple-element.12), channel_id=1, source_target_pairs={{0,128},{64,192},{128,256},{192,320},{256,384},{320,448},{384,512}... | collective-permute-start | bytes 245768 | tf_op jit(solution)/shard_map/ppermute | solution.py:228
  68.5 0.0 collective-permute-done.1
  68.5 0.1 collective-permute-done.3
  68.6 7.9 %collective-permute-done.2 = f32[4,40,128]{2,1,0:T(8,128)S(1)} collective-permute-done((f32[4,40,128]{2,1,0:T(8,128)S(1)}, f32[4,40,128]{2,1,0:T(8,128)S(1)}, u32[]{:S(2)}, u32[]{:S(2)}) %collective-permute-start.2) | collective-permute-done | bytes 81952 | tf_op jit(solution)/shard_map/ppermute | solution.py:228
  76.5 0.7 fusion.2
  77.2 0.0 all-to-all-done.2
  77.2 5.2 %all-to-all-start.3 = ((f32[4,40,128]{2,1,0:T(8,128)}), f32[4,40,128]{2,1,0:T(8,128)S(1)}, u32[]{:S(2)}, u32[]{:S(2)}) async-start(f32[4,40,128]{2,1,0:T(8,128)} %fusion.2), calls=%async_computation.3 | async-start | bytes 163840 | tf_op jit(solution)/shard_map/all_to_all | solution.py:237
  82.4 0.7 dynamic-slice_bitcast_fusion.rows_ref
  83.1 0.4 copy.9
  83.5 0.0 copy-done
  83.5 2.9 %modes_to_rows.1 = bf16[24,32,1024]{2,1,0:T(8,128)(2,1)} custom-call(f32[24,64,128]{2,1,0:T(8,128)S(1)} %bitcast.26, bf16[32,384]{1,0:T(8,128)(2,1)S(1)} %dynamic-slice_bitcast_fusion.rows_ref, bf16[384,1024]{1,0:T(8,128)(2,1)S(1)} %copy-done), custom_call_target="tpu_custom_call" | custom-call | tf_op jit(solution)/shard_map/modes_to_rows/pallas_call | solution.py:146
  86.5 10.1 %all-to-all-done.3 = f32[4,40,128]{2,1,0:T(8,128)S(1)} async-done(((f32[4,40,128]{2,1,0:T(8,128)}), f32[4,40,128]{2,1,0:T(8,128)S(1)}, u32[]{:S(2)}, u32[]{:S(2)}) %all-to-all-start.3) | async-done | bytes 81952 | tf_op jit(solution)/shard_map/all_to_all | solution.py:237
  96.6 0.6 slice_reduce_fusion
  (2 shorter events, 0.1 us)
Async XLA Ops:
  4.0 35.9 %copy-start.1 = (f32[2,24,24,128]{3,2,1,0:T(8,128)S(1)}, f32[2,24,24,128]{3,2,1,0:T(8,128)}, u32[]{:S(2)}) copy-start(f32[2,24,24,128]{3,2,1,0:T(8,128)} %weights_ref.1) | copy-start | bytes 1769476
  4.0 35.9 %copy-start.2 = (f32[2,1,24,128]{3,2,1,0:T(8,128)S(1)}, f32[2,1,24,128]{3,2,1,0:T(8,128)}, u32[]{:S(2)}) copy-start(f32[2,1,24,128]{3,2,1,0:T(8,128)} %param.8) | copy-start | bytes 73732
  41.3 35.9 %all-to-all-start.2 = ((f32[32,48,128]{2,1,0:T(8,128)}), f32[32,48,128]{2,1,0:T(8,128)S(1)}, u32[]{:S(2)}, u32[]{:S(2)}) async-start(f32[32,48,128]{2,1,0:T(8,128)} %get-tuple-element.6), calls=%async_computation.2 | async-start | bytes 1572864 | tf_op jit(solution)/shard_map/all_to_all | solution.py:252
  46.3 3.5 %collective-permute-start = (f32[4,4,40,128]{3,2,1,0:T(8,128)S(1)}, f32[4,4,40,128]{3,2,1,0:T(8,128)S(1)}, u32[]{:S(2)}, u32[]{:S(2)}) collective-permute-start(f32[4,4,40,128]{3,2,1,0:T(8,128)S(1)} %get-tuple-element.8), channel_id=1, source_target_pairs={{0,32},{32,0},{1,33},{33,1},{2,34},{34,2},{3,35},{35,3},{4,36},{36... | collective-permute-start | bytes 983048 | tf_op jit(solution)/shard_map/ppermute | solution.py:232
  49.9 33.6 %copy-start = (bf16[384,1024]{1,0:T(8,128)(2,1)S(1)}, bf16[384,1024]{1,0:T(8,128)(2,1)}, u32[]{:S(2)}) copy-start(bf16[384,1024]{1,0:T(8,128)(2,1)} %constant.29.clone.basis_ref) | copy-start | bytes 2359300
  49.9 18.6 %collective-permute-start.1 = (f32[4,40,128]{2,1,0:T(8,128)S(1)}, f32[4,40,128]{2,1,0:T(8,128)S(1)}, u32[]{:S(2)}, u32[]{:S(2)}) collective-permute-start(f32[4,40,128]{2,1,0:T(8,128)S(1)} %get-tuple-element.10), channel_id=1, source_target_pairs={{0,64},{64,128},{128,192},{192,256},{256,320},{320,384},{384,448},... | collective-permute-start | bytes 245768 | tf_op jit(solution)/shard_map/ppermute | solution.py:228
  52.0 16.6 %collective-permute-start.3 = (f32[4,40,128]{2,1,0:T(8,128)S(1)}, f32[4,40,128]{2,1,0:T(8,128)S(1)}, u32[]{:S(2)}, u32[]{:S(2)}) collective-permute-start(f32[4,40,128]{2,1,0:T(8,128)S(1)} %get-tuple-element.11), channel_id=1, source_target_pairs={{0,960},{64,0},{128,64},{192,128},{256,192},{320,256},{384,320},{4... | collective-permute-start | bytes 245768 | tf_op jit(solution)/shard_map/ppermute | solution.py:228
  66.5 10.0 %collective-permute-start.2 = (f32[4,40,128]{2,1,0:T(8,128)S(1)}, f32[4,40,128]{2,1,0:T(8,128)S(1)}, u32[]{:S(2)}, u32[]{:S(2)}) collective-permute-start(f32[4,40,128]{2,1,0:T(8,128)S(1)} %get-tuple-element.12), channel_id=1, source_target_pairs={{0,128},{64,192},{128,256},{192,320},{256,384},{320,448},{384,512}... | collective-permute-start | bytes 245768 | tf_op jit(solution)/shard_map/ppermute | solution.py:228
  77.2 19.4 %all-to-all-start.3 = ((f32[4,40,128]{2,1,0:T(8,128)}), f32[4,40,128]{2,1,0:T(8,128)S(1)}, u32[]{:S(2)}, u32[]{:S(2)}) async-start(f32[4,40,128]{2,1,0:T(8,128)} %fusion.2), calls=%async_computation.3 | async-start | bytes 163840 | tf_op jit(solution)/shard_map/all_to_all | solution.py:237

commit v6 on v5

--- a/solution.py
+++ b/solution.py
@@ -105,7 +105,7 @@
     table = np.concatenate(row_tables(modes_x, row_count, height), axis=2) / math.sqrt(height * col_count)
     high, low = halves(table)
     rows = np.concatenate([high, high, low], axis=2)
-    chunks = 3
+    chunks = 1
     return pl.pallas_call(
         forward_kernel,
         out_shape=jax.ShapeDtypeStruct((modes_x, channels, 2 * modes_y), jnp.float32),
@@ -231,7 +231,7 @@
 def sum_to_owners(mine, other, later):
     mine = mine + lax.ppermute(other, "core", [(0, 1), (1, 0)])
     total = mine[0]
-    for ahead in range(1, mine.shape[0]):
+    for ahead in (2, 1, 3):
         total = total + shift(mine[ahead], HOPS[ahead])
     total, _ = lax.optimization_barrier((total, later))
     return lax.all_to_all(total, "far", 0, 0, tiled=True)

time: 97.8 us -> 96.4 us (0.986)
  waiting for transfers between devices: 19.7 us -> 16.6 us
  starting transfers between devices: 30.7 us -> 33.1 us
    ppermute x3, waiting for transfers between devices: 8.03 us -> 5.61 us  [shift(): lax.ppermute(x, ('far', 'near'), [(z, (z + hop) % chips) for z in range(c...]
    all_to_all x1, starting transfers between devices: 5.18 us -> 7.6 us  [sum_to_owners(): return lax.all_to_all(total, 'far', 0, 0, tiled=True)]
where the time goes in v6:
time: 96.4 us; the launch traced here: 95.9 us
  blocking collectives  35.8 us (37%)
  starting transfers between devices  33.1 us (34%)
  waiting for transfers between devices  16.6 us (17%)
  Pallas kernels  7.02 us (7%)
  other arithmetic  1.38 us (1%)
  local copies, waits for them, and re-layouts  1.19 us (1%)
    all_to_all x1, blocking collectives, body(): partial = lax.all_to_all(partial, 'column', 0, 0, tiled=True)  19.3 us
    ppermute x3, starting transfers between devices, shift(): lax.ppermute(x, ('far', 'near'), [(z, (z + hop) % chips) for z in range(c...  18.5 us
    all_to_all x1, blocking collectives, body(): partial = lax.all_to_all(partial, 'row', 0, 0, tiled=True)  16.5 us
    all_to_all x1, waiting for transfers between devices, sum_to_owners(): return lax.all_to_all(total, 'far', 0, 0, tiled=True)  9.39 us
    all_to_all x1, starting transfers between devices, sum_to_owners(): return lax.all_to_all(total, 'far', 0, 0, tiled=True)  7.6 us
    ppermute x3, waiting for transfers between devices, shift(): lax.ppermute(x, ('far', 'near'), [(z, (z + hop) % chips) for z in range(c...  5.61 us
    all_to_all x1, starting transfers between devices, body(): all_spec = lax.all_to_all(everyone, SPACE, 0, 0, tiled=True)  5.02 us
    pallas_call x1, Pallas kernels, inverse(): pl.pallas_call(inverse_kernel, grid=(channels // step,), out_shape=jax.Sh...  2.94 us
  transfers between devices with their start and end apart: 6, of which 4 were waited for; matrix products, arithmetic and copies ran while one was open for 2% of the time, Pallas kernels for 3%

profile of v6, /device:TPU:8, one launch (start us, length us, event | category | flops | bytes accessed | tf_op | source)
XLA Modules:
  0.0 95.9 jit_solution(13799028746591870491)
XLA Ops:
  0.6 2.7 %rows_to_modes.1 = f32[64,24,128]{2,1,0:T(8,128)S(1)} custom-call(bf16[24,32,1024]{2,1,0:T(8,128)(2,1)} %bitcast.31, bf16[1024,256]{1,0:T(8,128)(2,1)} %constant.26.clone.basis_hbm, bf16[32,64,192]{2,1,0:T(8,128)(2,1)} %constant.27.clone.rows_hbm), custom_call_target="tpu_custom_call" | custom-call | tf_op jit(solution)/shard_map/rows_to_modes/pallas_call | solution.py:109
  3.4 0.0 copy-start.1
  3.4 0.0 copy-start.2
  3.4 16.5 %all_to_all.20 = f32[64,24,128]{2,1,0:T(8,128)S(1)} all-to-all(f32[64,24,128]{2,1,0:T(8,128)S(1)} %rows_to_modes.1), channel_id=1, replica_groups=mesh['far'=4,'near'=4,'core'=2,'row'=4,'column'=8] {'row'}, dimensions={0} | all-to-all | bytes 1572864 | tf_op jit(solution)/shard_map/all_to_all | solution.py:248
  19.9 19.3 %all_to_all.21.got_ref = f32[16,24,128]{2,1,0:T(8,128)S(1)} all-to-all(f32[16,24,128]{2,1,0:T(8,128)S(1)} %reduce_sum.18), channel_id=1, replica_groups=mesh['far'=4,'near'=4,'core'=2,'row'=4,'column'=8] {'column'}, dimensions={0} | all-to-all | bytes 393216 | tf_op jit(solution)/shard_map/all_to_all | solution.py:250
  39.3 0.0 copy-done.1
  39.3 0.0 copy-done.2
  39.3 1.3 %modes.1 = (f32[32,48,128]{2,1,0:T(8,128)}, f32[4,4,40,128]{3,2,1,0:T(8,128)S(1)}, f32[4,4,40,128]{3,2,1,0:T(8,128)S(1)}) custom-call(f32[16,24,128]{2,1,0:T(8,128)S(1)} %all_to_all.21.got_ref, f32[2,24,24,128]{3,2,1,0:T(8,128)S(1)} %copy-done.1, f32[2,24,128]{2,1,0:T(8,128)S(1)} %bitcast.27), custom_call_target="tpu_custom_call" | custom-call | tf_op jit(solution)/shard_map/modes/pallas_call | solution.py:211
  40.6 5.0 %all-to-all-start.2 = ((f32[32,48,128]{2,1,0:T(8,128)}), f32[32,48,128]{2,1,0:T(8,128)S(1)}, u32[]{:S(2)}, u32[]{:S(2)}) async-start(f32[32,48,128]{2,1,0:T(8,128)} %get-tuple-element.6), calls=%async_computation.2 | async-start | bytes 1572864 | tf_op jit(solution)/shard_map/all_to_all | solution.py:252
  45.7 1.9 %collective-permute-start = (f32[4,4,40,128]{3,2,1,0:T(8,128)S(1)}, f32[4,4,40,128]{3,2,1,0:T(8,128)S(1)}, u32[]{:S(2)}, u32[]{:S(2)}) collective-permute-start(f32[4,4,40,128]{3,2,1,0:T(8,128)S(1)} %get-tuple-element.8), channel_id=1, source_target_pairs={{0,32},{32,0},{1,33},{33,1},{2,34},{34,2},{3,35},{35,3},{4,36},{36... | collective-permute-start | bytes 983048 | tf_op jit(solution)/shard_map/ppermute | solution.py:232
  47.6 1.6 %collective-permute-done = f32[4,4,40,128]{3,2,1,0:T(8,128)S(1)} collective-permute-done((f32[4,4,40,128]{3,2,1,0:T(8,128)S(1)}, f32[4,4,40,128]{3,2,1,0:T(8,128)S(1)}, u32[]{:S(2)}, u32[]{:S(2)}) %collective-permute-start) | collective-permute-done | bytes 327712 | tf_op jit(solution)/shard_map/ppermute | solution.py:232
  49.2 0.1 add.21
  49.2 0.0 copy-start
  49.3 2.6 %collective-permute-start.1 = (f32[4,40,128]{2,1,0:T(8,128)S(1)}, f32[4,40,128]{2,1,0:T(8,128)S(1)}, u32[]{:S(2)}, u32[]{:S(2)}) collective-permute-start(f32[4,40,128]{2,1,0:T(8,128)S(1)} %get-tuple-element.10), channel_id=1, source_target_pairs={{0,128},{64,192},{128,256},{192,320},{256,384},{320,448},{384,512}... | collective-permute-start | bytes 245768 | tf_op jit(solution)/shard_map/ppermute | solution.py:228
  51.8 14.1 %collective-permute-start.3 = (f32[4,40,128]{2,1,0:T(8,128)S(1)}, f32[4,40,128]{2,1,0:T(8,128)S(1)}, u32[]{:S(2)}, u32[]{:S(2)}) collective-permute-start(f32[4,40,128]{2,1,0:T(8,128)S(1)} %get-tuple-element.11), channel_id=1, source_target_pairs={{0,960},{64,0},{128,64},{192,128},{256,192},{320,256},{384,320},{4... | collective-permute-start | bytes 245768 | tf_op jit(solution)/shard_map/ppermute | solution.py:228
  65.9 1.9 %collective-permute-start.2 = (f32[4,40,128]{2,1,0:T(8,128)S(1)}, f32[4,40,128]{2,1,0:T(8,128)S(1)}, u32[]{:S(2)}, u32[]{:S(2)}) collective-permute-start(f32[4,40,128]{2,1,0:T(8,128)S(1)} %get-tuple-element.12), channel_id=1, source_target_pairs={{0,64},{64,128},{128,192},{192,256},{256,320},{320,384},{384,448},... | collective-permute-start | bytes 245768 | tf_op jit(solution)/shard_map/ppermute | solution.py:228
  67.8 0.0 collective-permute-done.1
  67.8 0.1 collective-permute-done.3
  67.9 5.5 %collective-permute-done.2 = f32[4,40,128]{2,1,0:T(8,128)S(1)} collective-permute-done((f32[4,40,128]{2,1,0:T(8,128)S(1)}, f32[4,40,128]{2,1,0:T(8,128)S(1)}, u32[]{:S(2)}, u32[]{:S(2)}) %collective-permute-start.2) | collective-permute-done | bytes 81952 | tf_op jit(solution)/shard_map/ppermute | solution.py:228
  73.5 0.7 fusion.2
  74.1 0.0 all-to-all-done.2
  74.1 7.6 %all-to-all-start.3 = ((f32[4,40,128]{2,1,0:T(8,128)}), f32[4,40,128]{2,1,0:T(8,128)S(1)}, u32[]{:S(2)}, u32[]{:S(2)}) async-start(f32[4,40,128]{2,1,0:T(8,128)} %fusion.2), calls=%async_computation.3 | async-start | bytes 163840 | tf_op jit(solution)/shard_map/all_to_all | solution.py:237
  81.7 0.7 dynamic-slice_bitcast_fusion.rows_ref
  82.5 0.4 copy.9
  82.9 0.0 copy-done
  82.9 2.9 %modes_to_rows.1 = bf16[24,32,1024]{2,1,0:T(8,128)(2,1)} custom-call(f32[24,64,128]{2,1,0:T(8,128)S(1)} %bitcast.26, bf16[32,384]{1,0:T(8,128)(2,1)S(1)} %dynamic-slice_bitcast_fusion.rows_ref, bf16[384,1024]{1,0:T(8,128)(2,1)S(1)} %copy-done), custom_call_target="tpu_custom_call" | custom-call | tf_op jit(solution)/shard_map/modes_to_rows/pallas_call | solution.py:146
  85.8 9.4 %all-to-all-done.3 = f32[4,40,128]{2,1,0:T(8,128)S(1)} async-done(((f32[4,40,128]{2,1,0:T(8,128)}), f32[4,40,128]{2,1,0:T(8,128)S(1)}, u32[]{:S(2)}, u32[]{:S(2)}) %all-to-all-start.3) | async-done | bytes 81952 | tf_op jit(solution)/shard_map/all_to_all | solution.py:237
  95.2 0.6 slice_reduce_fusion
  (2 shorter events, 0.1 us)
Async XLA Ops:
  3.4 35.9 %copy-start.1 = (f32[2,24,24,128]{3,2,1,0:T(8,128)S(1)}, f32[2,24,24,128]{3,2,1,0:T(8,128)}, u32[]{:S(2)}) copy-start(f32[2,24,24,128]{3,2,1,0:T(8,128)} %weights_ref.1) | copy-start | bytes 1769476
  3.4 35.9 %copy-start.2 = (f32[2,1,24,128]{3,2,1,0:T(8,128)S(1)}, f32[2,1,24,128]{3,2,1,0:T(8,128)}, u32[]{:S(2)}) copy-start(f32[2,1,24,128]{3,2,1,0:T(8,128)} %param.8) | copy-start | bytes 73732
  40.6 33.5 %all-to-all-start.2 = ((f32[32,48,128]{2,1,0:T(8,128)}), f32[32,48,128]{2,1,0:T(8,128)S(1)}, u32[]{:S(2)}, u32[]{:S(2)}) async-start(f32[32,48,128]{2,1,0:T(8,128)} %get-tuple-element.6), calls=%async_computation.2 | async-start | bytes 1572864 | tf_op jit(solution)/shard_map/all_to_all | solution.py:252
  45.7 3.5 %collective-permute-start = (f32[4,4,40,128]{3,2,1,0:T(8,128)S(1)}, f32[4,4,40,128]{3,2,1,0:T(8,128)S(1)}, u32[]{:S(2)}, u32[]{:S(2)}) collective-permute-start(f32[4,4,40,128]{3,2,1,0:T(8,128)S(1)} %get-tuple-element.8), channel_id=1, source_target_pairs={{0,32},{32,0},{1,33},{33,1},{2,34},{34,2},{3,35},{35,3},{4,36},{36... | collective-permute-start | bytes 983048 | tf_op jit(solution)/shard_map/ppermute | solution.py:232
  49.2 33.6 %copy-start = (bf16[384,1024]{1,0:T(8,128)(2,1)S(1)}, bf16[384,1024]{1,0:T(8,128)(2,1)}, u32[]{:S(2)}) copy-start(bf16[384,1024]{1,0:T(8,128)(2,1)} %constant.29.clone.basis_ref) | copy-start | bytes 2359300
  49.3 18.6 %collective-permute-start.1 = (f32[4,40,128]{2,1,0:T(8,128)S(1)}, f32[4,40,128]{2,1,0:T(8,128)S(1)}, u32[]{:S(2)}, u32[]{:S(2)}) collective-permute-start(f32[4,40,128]{2,1,0:T(8,128)S(1)} %get-tuple-element.10), channel_id=1, source_target_pairs={{0,128},{64,192},{128,256},{192,320},{256,384},{320,448},{384,512}... | collective-permute-start | bytes 245768 | tf_op jit(solution)/shard_map/ppermute | solution.py:228
  51.8 16.1 %collective-permute-start.3 = (f32[4,40,128]{2,1,0:T(8,128)S(1)}, f32[4,40,128]{2,1,0:T(8,128)S(1)}, u32[]{:S(2)}, u32[]{:S(2)}) collective-permute-start(f32[4,40,128]{2,1,0:T(8,128)S(1)} %get-tuple-element.11), channel_id=1, source_target_pairs={{0,960},{64,0},{128,64},{192,128},{256,192},{320,256},{384,320},{4... | collective-permute-start | bytes 245768 | tf_op jit(solution)/shard_map/ppermute | solution.py:228
  65.9 7.5 %collective-permute-start.2 = (f32[4,40,128]{2,1,0:T(8,128)S(1)}, f32[4,40,128]{2,1,0:T(8,128)S(1)}, u32[]{:S(2)}, u32[]{:S(2)}) collective-permute-start(f32[4,40,128]{2,1,0:T(8,128)S(1)} %get-tuple-element.12), channel_id=1, source_target_pairs={{0,64},{64,128},{128,192},{192,256},{256,320},{320,384},{384,448},... | collective-permute-start | bytes 245768 | tf_op jit(solution)/shard_map/ppermute | solution.py:228
  74.1 21.1 %all-to-all-start.3 = ((f32[4,40,128]{2,1,0:T(8,128)}), f32[4,40,128]{2,1,0:T(8,128)S(1)}, u32[]{:S(2)}, u32[]{:S(2)}) async-start(f32[4,40,128]{2,1,0:T(8,128)} %fusion.2), calls=%async_computation.3 | async-start | bytes 163840 | tf_op jit(solution)/shard_map/all_to_all | solution.py:237

commit v7 on v6

--- a/solution.py
+++ b/solution.py
@@ -15,6 +15,7 @@
 SPACE = ("row", "column")
 FAR = 4
 ROWS = 4
+SENDS = 4
 HOPS = (0, 1, 2, -1)
 VMEM = pl.BlockSpec(memory_space=pltpu.VMEM)
 HBM = pl.BlockSpec(memory_space=pltpu.HBM)
@@ -154,7 +155,7 @@
     )(all_spec, rows, jnp.asarray(basis))
 
 
-def middle_kernel(got_ref, weights_ref, spectrum_ref, spec_ref, mine_ref, other_ref, one_ref, terms_ref):
+def middle_kernel(got_ref, weights_ref, spectrum_ref, spec_hbm, mine_ref, other_ref, one_ref, copies_ref, terms_ref, sems):
     modes, channels, width = spectrum_ref.shape
     half = width // 2
     here, core = lax.axis_index("near"), lax.axis_index("core")
@@ -176,8 +177,15 @@
         imag_part = pltpu.roll(crossed, half, 1) - crossed
         one_ref[pl.ds(k, channels, stride=modes), :] = jnp.where(left, real_part, imag_part)
     one = one_ref[...]
-    for s in range(spec_ref.shape[0]):
-        spec_ref[s] = one
+    batch = copies_ref.shape[0]
+    for s in range(batch):
+        copies_ref[s] = one
+    sends = [
+        pltpu.make_async_copy(copies_ref, spec_hbm.at[pl.ds(i * batch, batch)], sems.at[i])
+        for i in range(sems.shape[0])
+    ]
+    for send in sends:
+        send.start()
 
     for k in range(modes):
         own = spectrum_ref[k]
@@ -200,6 +208,8 @@
             one = terms_ref[pl.ds(first + owned, rows), :]
             mine_ref[ahead, target] = jnp.where(core == 0, zero, one)
             other_ref[ahead, target] = jnp.where(core == 0, one, zero)
+    for send in sends:
+        send.wait()
 
 
 def middle(got, weights, spectrum, copies):
@@ -212,10 +222,12 @@
         middle_kernel,
         out_shape=(jax.ShapeDtypeStruct((copies, channels * modes, width), jnp.float32), terms, terms),
         in_specs=[VMEM, VMEM, VMEM],
-        out_specs=(VMEM, VMEM, VMEM),
+        out_specs=(HBM, VMEM, VMEM),
         scratch_shapes=[
             pltpu.VMEM((channels * modes, width), jnp.float32),
+            pltpu.VMEM((copies // SENDS, channels * modes, width), jnp.float32),
             pltpu.VMEM((channels * channels * modes + 8, width), jnp.float32),
+            pltpu.SemaphoreType.DMA((SENDS,)),
         ],
         compiler_params=PARAMS,
         name="modes",

time: 96.4 us -> 96.5 us (level)
  no operation moved by 1% of the time
where the time goes in v7:
time: 96.5 us; the launch traced here: 95.9 us
  blocking collectives  35.8 us (37%)
  starting transfers between devices  33.1 us (34%)
  waiting for transfers between devices  16.6 us (17%)
  Pallas kernels  7.02 us (7%)
  other arithmetic  1.38 us (1%)
  local copies, waits for them, and re-layouts  1.19 us (1%)
    all_to_all x1, blocking collectives, body(): partial = lax.all_to_all(partial, 'column', 0, 0, tiled=True)  19.3 us
    ppermute x3, starting transfers between devices, shift(): lax.ppermute(x, ('far', 'near'), [(z, (z + hop) % chips) for z in range(c...  18.5 us
    all_to_all x1, blocking collectives, body(): partial = lax.all_to_all(partial, 'row', 0, 0, tiled=True)  16.5 us
    all_to_all x1, waiting for transfers between devices, sum_to_owners(): return lax.all_to_all(total, 'far', 0, 0, tiled=True)  9.39 us
    all_to_all x1, starting transfers between devices, sum_to_owners(): return lax.all_to_all(total, 'far', 0, 0, tiled=True)  7.6 us
    ppermute x3, waiting for transfers between devices, shift(): lax.ppermute(x, ('far', 'near'), [(z, (z + hop) % chips) for z in range(c...  5.61 us
    all_to_all x1, starting transfers between devices, body(): all_spec = lax.all_to_all(everyone, SPACE, 0, 0, tiled=True)  5.03 us
    pallas_call x1, Pallas kernels, inverse(): pl.pallas_call(inverse_kernel, grid=(channels // step,), out_shape=jax.Sh...  2.94 us
  transfers between devices with their start and end apart: 6, of which 4 were waited for; matrix products, arithmetic and copies ran while one was open for 2% of the time, Pallas kernels for 3%

profile of v7, /device:TPU:8, one launch (start us, length us, event | category | flops | bytes accessed | tf_op | source)
XLA Modules:
  0.0 95.9 jit_solution(8051120994775660410)
XLA Ops:
  0.6 2.7 %rows_to_modes.1 = f32[64,24,128]{2,1,0:T(8,128)S(1)} custom-call(bf16[24,32,1024]{2,1,0:T(8,128)(2,1)} %bitcast.31, bf16[1024,256]{1,0:T(8,128)(2,1)} %constant.26.clone.basis_hbm, bf16[32,64,192]{2,1,0:T(8,128)(2,1)} %constant.27.clone.rows_hbm), custom_call_target="tpu_custom_call" | custom-call | tf_op jit(solution)/shard_map/rows_to_modes/pallas_call | solution.py:110
  3.4 0.0 copy-start.1
  3.4 0.0 copy-start.2
  3.4 16.5 %all_to_all.20 = f32[64,24,128]{2,1,0:T(8,128)S(1)} all-to-all(f32[64,24,128]{2,1,0:T(8,128)S(1)} %rows_to_modes.1), channel_id=1, replica_groups=mesh['far'=4,'near'=4,'core'=2,'row'=4,'column'=8] {'row'}, dimensions={0} | all-to-all | bytes 1572864 | tf_op jit(solution)/shard_map/all_to_all | solution.py:260
  19.9 19.3 %all_to_all.21.got_ref = f32[16,24,128]{2,1,0:T(8,128)S(1)} all-to-all(f32[16,24,128]{2,1,0:T(8,128)S(1)} %reduce_sum.18), channel_id=1, replica_groups=mesh['far'=4,'near'=4,'core'=2,'row'=4,'column'=8] {'column'}, dimensions={0} | all-to-all | bytes 393216 | tf_op jit(solution)/shard_map/all_to_all | solution.py:262
  39.3 0.0 copy-done.1
  39.3 0.0 copy-done.2
  39.3 1.3 %modes.1 = (f32[32,48,128]{2,1,0:T(8,128)}, f32[4,4,40,128]{3,2,1,0:T(8,128)S(1)}, f32[4,4,40,128]{3,2,1,0:T(8,128)S(1)}) custom-call(f32[16,24,128]{2,1,0:T(8,128)S(1)} %all_to_all.21.got_ref, f32[2,24,24,128]{3,2,1,0:T(8,128)S(1)} %copy-done.1, f32[2,24,128]{2,1,0:T(8,128)S(1)} %bitcast.27), custom_call_target="tpu_custom_call" | custom-call | tf_op jit(solution)/shard_map/modes/pallas_call | solution.py:221
  40.6 5.0 %all-to-all-start.2 = ((f32[32,48,128]{2,1,0:T(8,128)}), f32[32,48,128]{2,1,0:T(8,128)S(1)}, u32[]{:S(2)}, u32[]{:S(2)}) async-start(f32[32,48,128]{2,1,0:T(8,128)} %get-tuple-element.6), calls=%async_computation.2 | async-start | bytes 1572864 | tf_op jit(solution)/shard_map/all_to_all | solution.py:264
  45.7 1.9 %collective-permute-start = (f32[4,4,40,128]{3,2,1,0:T(8,128)S(1)}, f32[4,4,40,128]{3,2,1,0:T(8,128)S(1)}, u32[]{:S(2)}, u32[]{:S(2)}) collective-permute-start(f32[4,4,40,128]{3,2,1,0:T(8,128)S(1)} %get-tuple-element.8), channel_id=1, source_target_pairs={{0,32},{32,0},{1,33},{33,1},{2,34},{34,2},{3,35},{35,3},{4,36},{36... | collective-permute-start | bytes 983048 | tf_op jit(solution)/shard_map/ppermute | solution.py:244
  47.6 1.6 %collective-permute-done = f32[4,4,40,128]{3,2,1,0:T(8,128)S(1)} collective-permute-done((f32[4,4,40,128]{3,2,1,0:T(8,128)S(1)}, f32[4,4,40,128]{3,2,1,0:T(8,128)S(1)}, u32[]{:S(2)}, u32[]{:S(2)}) %collective-permute-start) | collective-permute-done | bytes 327712 | tf_op jit(solution)/shard_map/ppermute | solution.py:244
  49.2 0.1 add.21
  49.3 0.0 copy-start
  49.3 2.6 %collective-permute-start.1 = (f32[4,40,128]{2,1,0:T(8,128)S(1)}, f32[4,40,128]{2,1,0:T(8,128)S(1)}, u32[]{:S(2)}, u32[]{:S(2)}) collective-permute-start(f32[4,40,128]{2,1,0:T(8,128)S(1)} %get-tuple-element.10), channel_id=1, source_target_pairs={{0,128},{64,192},{128,256},{192,320},{256,384},{320,448},{384,512}... | collective-permute-start | bytes 245768 | tf_op jit(solution)/shard_map/ppermute | solution.py:240
  51.9 14.1 %collective-permute-start.3 = (f32[4,40,128]{2,1,0:T(8,128)S(1)}, f32[4,40,128]{2,1,0:T(8,128)S(1)}, u32[]{:S(2)}, u32[]{:S(2)}) collective-permute-start(f32[4,40,128]{2,1,0:T(8,128)S(1)} %get-tuple-element.11), channel_id=1, source_target_pairs={{0,960},{64,0},{128,64},{192,128},{256,192},{320,256},{384,320},{4... | collective-permute-start | bytes 245768 | tf_op jit(solution)/shard_map/ppermute | solution.py:240
  65.9 1.9 %collective-permute-start.2 = (f32[4,40,128]{2,1,0:T(8,128)S(1)}, f32[4,40,128]{2,1,0:T(8,128)S(1)}, u32[]{:S(2)}, u32[]{:S(2)}) collective-permute-start(f32[4,40,128]{2,1,0:T(8,128)S(1)} %get-tuple-element.12), channel_id=1, source_target_pairs={{0,64},{64,128},{128,192},{192,256},{256,320},{320,384},{384,448},... | collective-permute-start | bytes 245768 | tf_op jit(solution)/shard_map/ppermute | solution.py:240
  67.8 0.0 collective-permute-done.1
  67.9 0.1 collective-permute-done.3
  68.0 5.5 %collective-permute-done.2 = f32[4,40,128]{2,1,0:T(8,128)S(1)} collective-permute-done((f32[4,40,128]{2,1,0:T(8,128)S(1)}, f32[4,40,128]{2,1,0:T(8,128)S(1)}, u32[]{:S(2)}, u32[]{:S(2)}) %collective-permute-start.2) | collective-permute-done | bytes 81952 | tf_op jit(solution)/shard_map/ppermute | solution.py:240
  73.5 0.7 fusion.2
  74.1 0.0 all-to-all-done.2
  74.1 7.6 %all-to-all-start.3 = ((f32[4,40,128]{2,1,0:T(8,128)}), f32[4,40,128]{2,1,0:T(8,128)S(1)}, u32[]{:S(2)}, u32[]{:S(2)}) async-start(f32[4,40,128]{2,1,0:T(8,128)} %fusion.2), calls=%async_computation.3 | async-start | bytes 163840 | tf_op jit(solution)/shard_map/all_to_all | solution.py:249
  81.7 0.7 dynamic-slice_bitcast_fusion.rows_ref
  82.5 0.4 copy.9
  82.9 0.0 copy-done
  82.9 2.9 %modes_to_rows.1 = bf16[24,32,1024]{2,1,0:T(8,128)(2,1)} custom-call(f32[24,64,128]{2,1,0:T(8,128)S(1)} %bitcast.26, bf16[32,384]{1,0:T(8,128)(2,1)S(1)} %dynamic-slice_bitcast_fusion.rows_ref, bf16[384,1024]{1,0:T(8,128)(2,1)S(1)} %copy-done), custom_call_target="tpu_custom_call" | custom-call | tf_op jit(solution)/shard_map/modes_to_rows/pallas_call | solution.py:147
  85.8 9.4 %all-to-all-done.3 = f32[4,40,128]{2,1,0:T(8,128)S(1)} async-done(((f32[4,40,128]{2,1,0:T(8,128)}), f32[4,40,128]{2,1,0:T(8,128)S(1)}, u32[]{:S(2)}, u32[]{:S(2)}) %all-to-all-start.3) | async-done | bytes 81952 | tf_op jit(solution)/shard_map/all_to_all | solution.py:249
  95.2 0.6 slice_reduce_fusion
  (2 shorter events, 0.1 us)
Async XLA Ops:
  3.4 35.9 %copy-start.1 = (f32[2,24,24,128]{3,2,1,0:T(8,128)S(1)}, f32[2,24,24,128]{3,2,1,0:T(8,128)}, u32[]{:S(2)}) copy-start(f32[2,24,24,128]{3,2,1,0:T(8,128)} %weights_ref.1) | copy-start | bytes 1769476
  3.4 35.9 %copy-start.2 = (f32[2,1,24,128]{3,2,1,0:T(8,128)S(1)}, f32[2,1,24,128]{3,2,1,0:T(8,128)}, u32[]{:S(2)}) copy-start(f32[2,1,24,128]{3,2,1,0:T(8,128)} %param.8) | copy-start | bytes 73732
  40.6 33.5 %all-to-all-start.2 = ((f32[32,48,128]{2,1,0:T(8,128)}), f32[32,48,128]{2,1,0:T(8,128)S(1)}, u32[]{:S(2)}, u32[]{:S(2)}) async-start(f32[32,48,128]{2,1,0:T(8,128)} %get-tuple-element.6), calls=%async_computation.2 | async-start | bytes 1572864 | tf_op jit(solution)/shard_map/all_to_all | solution.py:264
  45.7 3.5 %collective-permute-start = (f32[4,4,40,128]{3,2,1,0:T(8,128)S(1)}, f32[4,4,40,128]{3,2,1,0:T(8,128)S(1)}, u32[]{:S(2)}, u32[]{:S(2)}) collective-permute-start(f32[4,4,40,128]{3,2,1,0:T(8,128)S(1)} %get-tuple-element.8), channel_id=1, source_target_pairs={{0,32},{32,0},{1,33},{33,1},{2,34},{34,2},{3,35},{35,3},{4,36},{36... | collective-permute-start | bytes 983048 | tf_op jit(solution)/shard_map/ppermute | solution.py:244
  49.3 33.6 %copy-start = (bf16[384,1024]{1,0:T(8,128)(2,1)S(1)}, bf16[384,1024]{1,0:T(8,128)(2,1)}, u32[]{:S(2)}) copy-start(bf16[384,1024]{1,0:T(8,128)(2,1)} %constant.29.clone.basis_ref) | copy-start | bytes 2359300
  49.3 18.6 %collective-permute-start.1 = (f32[4,40,128]{2,1,0:T(8,128)S(1)}, f32[4,40,128]{2,1,0:T(8,128)S(1)}, u32[]{:S(2)}, u32[]{:S(2)}) collective-permute-start(f32[4,40,128]{2,1,0:T(8,128)S(1)} %get-tuple-element.10), channel_id=1, source_target_pairs={{0,128},{64,192},{128,256},{192,320},{256,384},{320,448},{384,512}... | collective-permute-start | bytes 245768 | tf_op jit(solution)/shard_map/ppermute | solution.py:240
  51.9 16.1 %collective-permute-start.3 = (f32[4,40,128]{2,1,0:T(8,128)S(1)}, f32[4,40,128]{2,1,0:T(8,128)S(1)}, u32[]{:S(2)}, u32[]{:S(2)}) collective-permute-start(f32[4,40,128]{2,1,0:T(8,128)S(1)} %get-tuple-element.11), channel_id=1, source_target_pairs={{0,960},{64,0},{128,64},{192,128},{256,192},{320,256},{384,320},{4... | collective-permute-start | bytes 245768 | tf_op jit(solution)/shard_map/ppermute | solution.py:240
  65.9 7.5 %collective-permute-start.2 = (f32[4,40,128]{2,1,0:T(8,128)S(1)}, f32[4,40,128]{2,1,0:T(8,128)S(1)}, u32[]{:S(2)}, u32[]{:S(2)}) collective-permute-start(f32[4,40,128]{2,1,0:T(8,128)S(1)} %get-tuple-element.12), channel_id=1, source_target_pairs={{0,64},{64,128},{128,192},{192,256},{256,320},{320,384},{384,448},... | collective-permute-start | bytes 245768 | tf_op jit(solution)/shard_map/ppermute | solution.py:240
  74.1 21.1 %all-to-all-start.3 = ((f32[4,40,128]{2,1,0:T(8,128)}), f32[4,40,128]{2,1,0:T(8,128)S(1)}, u32[]{:S(2)}, u32[]{:S(2)}) async-start(f32[4,40,128]{2,1,0:T(8,128)} %fusion.2), calls=%async_computation.3 | async-start | bytes 163840 | tf_op jit(solution)/shard_map/all_to_all | solution.py:249
